TPU v7x, 512 devices: a whole 4x4x16 slice. The times are simulated.
512 devices in a mesh: section: 8 (over y, z_hi), dp: 16 (over z_lo, core), chan: 4 (over x).
Axes of the slice: x: 4, y: 4, z: 16 (z_hi: 2, z_lo: 8; z = z_hi * 8 + z_lo), core: 2. Of those that a mesh axis runs over, the one named last changes fastest.
Arguments:
- clips: bfloat16 [2, 512, 2048], P(None, 'chan', 'dp'), may hold values from -6 to 6
- weights: bfloat16 [8, 512, 27, 512], P('section', ('chan', 'dp')), may hold values from -0.0546875 to 0.0546875
- cotangents: bfloat16 [2, 512, 2048], P(None, 'chan', 'dp'), may hold values from -0.5 to 0.5
Outputs:
- weight_grads: float32 [8, 512, 27, 512], P('section', ('chan', 'dp'))
All inputs are finite; a program needn't handle non-finite values.
Results may differ from a plain program's by a relative error of at most 0.019.
Values may be sent and summed in bfloat16 or wider, within the bound.
No kernel may reach another device: no remote copies, remote signals or barrier semaphores. Data moves between devices by JAX's collectives and lax.ppermute only.
A program may use at most 128 MiB of HBM per device.

v0:
```python
import jax
import jax.numpy as jnp
from jax import lax
from jax.sharding import PartitionSpec as P

FRAMES = 4
HEIGHT = 4
WIDTH = 8
MICRO = 2


def from_partner(block, axis, distance):
    count = lax.axis_size(axis)
    route = []
    for low in range(count):
        high = low | 1 << distance
        if high != low and high < count:
            route += [(low, high), (high, low)]
    return lax.ppermute(block, axis, route)


def with_halo(shard, sides, width):
    for axis, dim in sides:
        size, length = (lax.axis_size(axis), shard.shape[dim])
        up = [(i, (i + 1) % size) for i in range(size - 1)]
        down = [(j, i) for i, j in up]
        last = lax.slice_in_dim(shard, length - width, length, axis=dim)
        first = lax.slice_in_dim(shard, 0, width, axis=dim)
        before = lax.ppermute(last, axis, up)
        after = lax.ppermute(first, axis, down)
        shard = jnp.concatenate([before, shard, after], axis=dim)
    return shard


def as_sent(shard):

    def short(part):
        return part.astype(jnp.bfloat16) if part.dtype == jnp.float32 else part

    return jax.tree.map(short, shard)


def silu_slope(values):
    sigmoid = jax.nn.sigmoid(values)
    return sigmoid * (1.0 + values * (1.0 - sigmoid))


def shifted_taps(source, time_shift, mirror, frames, height, columns):
    cell_count = source.shape[1]
    plane_size = height * columns
    margin = plane_size + columns + 1
    padded = jnp.pad(source, ((0, 0), (margin, margin)))
    position = jnp.arange(cell_count, dtype=jnp.int32)
    frame_of = position // plane_size % frames
    row_of = position // columns % height
    column_of = position % columns
    windows = []
    for row_shift in range(3):
        for column_shift in range(3):
            if mirror:
                move_frame, move_row, move_column = (
                    1 - time_shift,
                    1 - row_shift,
                    1 - column_shift,
                )
            else:
                move_frame, move_row, move_column = (
                    time_shift - 1,
                    row_shift - 1,
                    column_shift - 1,
                )
            offset = move_frame * plane_size + move_row * columns + move_column
            window = padded[:, margin + offset : margin + offset + cell_count]
            inside = (
                (frame_of + move_frame >= 0)
                & (frame_of + move_frame < frames)
                & (row_of + move_row >= 0)
                & (row_of + move_row < height)
                & (column_of + move_column >= 0)
                & (column_of + move_column < columns)
            )
            windows.append(jnp.where(inside[None, :], window, jnp.zeros_like(window)))
    return windows


def arrange_kernel(kernel):
    outputs = kernel.shape[0]
    inputs = kernel.shape[2]
    return kernel.reshape(outputs, 3, 9 * inputs).transpose(1, 0, 2)


def conv_forward(activated, arranged, frames, height, columns):
    outputs = arranged.shape[1]
    result = jnp.zeros((outputs, activated.shape[1]), jnp.float32)
    for time_shift in range(3):
        stacked = jnp.concatenate(
            shifted_taps(activated, time_shift, False, frames, height, columns), axis=0
        )
        result = result + jnp.dot(arranged[time_shift], stacked, preferred_element_type=jnp.float32)
    return result


def conv_input_grad(grads_all, arranged, frames, height, columns):
    outputs = arranged.shape[1]
    inputs = arranged.shape[2] // 9
    cell_count = grads_all.shape[1]
    result = jnp.zeros((inputs, cell_count), jnp.float32)
    for time_shift in range(3):
        stacked = jnp.stack(
            shifted_taps(grads_all, time_shift, True, frames, height, columns), axis=1
        )
        stacked = stacked.reshape(-1, cell_count)
        matrix = arranged[time_shift].reshape(outputs * 9, inputs)
        result = result + lax.dot_general(
            matrix, stacked, (((0,), (0,)), ((), ())), preferred_element_type=jnp.float32
        )
    return result


def weight_grad_from_grads(activated, grad_low, frames, height, columns):
    outputs = grad_low.shape[0]
    cell_count = grad_low.shape[1]
    pieces = []
    for time_shift in range(3):
        stacked = jnp.stack(
            shifted_taps(grad_low, time_shift, True, frames, height, columns), axis=1
        )
        stacked = stacked.reshape(outputs * 9, cell_count)
        product = lax.dot_general(
            stacked, activated, (((1,), (1,)), ((), ())), preferred_element_type=jnp.float32
        )
        pieces.append(product.reshape(outputs, 9, activated.shape[0]))
    return jnp.concatenate(pieces, axis=1)


def mirror_pair(source):
    for bit_index in range(lax.axis_size("section").bit_length() - 1):
        source = from_partner(source, "section", bit_index)
    return source


def kernel_mirror(source):
    for bit_index in range(lax.axis_size("section").bit_length() - 1):
        source = from_partner(source, "section", bit_index)
    return source


def mirror_grads(source):
    for bit_index in range(lax.axis_size("section").bit_length() - 1):
        source = from_partner(source.astype(jnp.bfloat16), "section", bit_index).astype(
            source.dtype
        )
    return source


def channel_gather(source):
    return lax.all_gather(source, "chan", axis=0, tiled=True)


def section_rims(source):
    return with_halo(source[None], (("section", 0),), 1)


def active_lane(tick_index, positions, spacing, per_lane, lane_count):
    offsets = tick_index - positions
    first_aligned = offsets[0] % spacing == 0
    lane_now = jnp.where(first_aligned, 0, lane_count - 1).astype(jnp.int32)
    offset = jnp.where(first_aligned, offsets[0], offsets[lane_count - 1])
    slot_now = offset // spacing
    is_valid = (offset % spacing == 0) & (slot_now >= 0) & (slot_now < per_lane)
    return (lane_now, jnp.clip(slot_now, 0, per_lane - 1), is_valid)


def store_slot(buffer, lane_now, slot_now, is_valid, payload):
    chosen = jnp.where(is_valid, payload, buffer[lane_now, slot_now])
    starts = (lane_now, slot_now) + (0,) * payload.ndim
    return lax.dynamic_update_slice(buffer, chosen[None, None], starts)


def receive_slots(buffer, anchors, keep_mask, tick_index, spacing, per_lane, payload):
    for lane_index in range(anchors.shape[0]):
        offset = tick_index - anchors[lane_index]
        slot_now = offset // spacing
        is_valid = (
            keep_mask[lane_index]
            & (offset % spacing == 0)
            & (slot_now >= 0)
            & (slot_now < per_lane)
        )
        buffer = store_slot(
            buffer, lane_index, jnp.clip(slot_now, 0, per_lane - 1), is_valid, payload
        )
    return buffer


def branch_index(is_valid, lane_now):
    return jnp.where(is_valid, lane_now + 1, 0)


def on_device(clips, weights, cotangents):
    sections = lax.axis_size("section")
    section_id = lax.axis_index("section")
    half_depth = sections // 2
    local_rows = clips.shape[1]
    cell_count = clips.shape[2]
    channels = local_rows * lax.axis_size("chan")
    own_share = weights[0]
    lane_shares = jnp.stack([own_share, kernel_mirror(own_share)])
    lane_layers = jnp.stack([section_id, sections - 1 - section_id])
    lane_first = jnp.array([0, MICRO // 2], jnp.int32)
    per_lane = MICRO // 2
    spacing = 2
    lane_count = lane_shares.shape[0]
    lane_kernels = lax.all_gather(lane_shares, "dp", axis=1, tiled=True)
    arranged_lanes = [arrange_kernel(lane_kernels[lane_index]) for lane_index in range(lane_count)]
    tick_count = sections + spacing * (per_lane - 1)

    def forward_tick(tick_index, carried):
        incoming, inputs_buf, skip_buf, acts_buf = carried
        lane_now, slot_now, is_valid = active_lane(
            tick_index, lane_layers, spacing, per_lane, lane_count
        )
        layer_now = lane_layers[lane_now]
        clip_now = clips[lane_first[lane_now] + slot_now]
        state_now = jnp.where(layer_now == 0, clip_now, incoming[lane_now])
        skip_now = skip_buf[lane_now, slot_now]
        summed = state_now.astype(jnp.float32) + skip_now.astype(jnp.float32)
        activated = jax.nn.silu(summed).astype(jnp.bfloat16)
        acts_all = channel_gather(activated)

        def forward_skipped():
            return jnp.zeros(state_now.shape, jnp.float32)

        def forward_make_branch(lane_index):

            def convolve():
                return conv_forward(acts_all, arranged_lanes[lane_index], FRAMES, HEIGHT, WIDTH)

            return convolve

        branches = [forward_skipped] + [
            forward_make_branch(lane_index) for lane_index in range(lane_count)
        ]
        update = lax.switch(branch_index(is_valid, lane_now), branches)
        output = (state_now.astype(jnp.float32) + update).astype(jnp.bfloat16)
        inputs_buf = store_slot(inputs_buf, lane_now, slot_now, is_valid, state_now)
        acts_buf = store_slot(acts_buf, lane_now, slot_now, is_valid, acts_all)
        outgoing = jnp.where(is_valid & (layer_now < half_depth), output, jnp.zeros_like(output))
        arrived = mirror_pair(outgoing)
        skip_buf = receive_slots(
            skip_buf,
            sections - 1 - lane_layers,
            lane_layers >= half_depth,
            tick_index,
            spacing,
            per_lane,
            arrived,
        )
        rim_rows = section_rims(output)
        incoming = jnp.stack([rim_rows[0], rim_rows[2]])
        return (incoming, inputs_buf, skip_buf, acts_buf)

    empty_rows = jnp.zeros((lane_count, local_rows, cell_count), jnp.bfloat16)
    empty_slots = jnp.zeros((lane_count, per_lane, local_rows, cell_count), jnp.bfloat16)
    empty_acts = jnp.zeros((lane_count, per_lane, channels, cell_count), jnp.bfloat16)
    forward_out = lax.fori_loop(
        0, tick_count, forward_tick, (empty_rows, empty_slots, empty_slots, empty_acts)
    )
    inputs_buf, skip_buf, acts_buf = (forward_out[1], forward_out[2], forward_out[3])

    def backward_tick(tick_index, carried):
        incoming, gskip_buf, glow_buf = carried
        lane_now, slot_now, is_valid = active_lane(
            tick_index, sections - 1 - lane_layers, spacing, per_lane, lane_count
        )
        layer_now = lane_layers[lane_now]
        cotangent_now = cotangents[lane_first[lane_now] + slot_now]
        upstream = jnp.where(layer_now == sections - 1, cotangent_now, incoming[lane_now]).astype(
            jnp.float32
        )
        upstream = upstream + gskip_buf[lane_now, slot_now].astype(jnp.float32)
        grad_low = upstream.astype(jnp.bfloat16)
        summed = inputs_buf[lane_now, slot_now].astype(jnp.float32) + skip_buf[
            lane_now, slot_now
        ].astype(jnp.float32)

        def backward_skipped():
            return jnp.zeros((channels, cell_count), jnp.float32)

        def backward_make_branch(lane_index):

            def differentiate():
                return conv_input_grad(grad_low, arranged_lanes[lane_index], FRAMES, HEIGHT, WIDTH)

            return differentiate

        branches = [backward_skipped] + [
            backward_make_branch(lane_index) for lane_index in range(lane_count)
        ]
        partial_terms = lax.switch(branch_index(is_valid, lane_now), branches)
        pre_grad = jax.tree.map(
            lambda part: part.astype(jnp.float32),
            lax.psum_scatter(as_sent(partial_terms), "chan", scatter_dimension=0, tiled=True),
        ) * silu_slope(summed)
        glow_buf = store_slot(glow_buf, lane_now, slot_now, is_valid, grad_low)
        sent = (upstream + pre_grad).astype(jnp.bfloat16)
        skip_low = pre_grad.astype(jnp.bfloat16)
        outgoing = jnp.where(
            is_valid & (layer_now >= half_depth), skip_low, jnp.zeros_like(skip_low)
        )
        arrived = mirror_pair(outgoing)
        gskip_buf = receive_slots(
            gskip_buf, lane_layers, lane_layers < half_depth, tick_index, spacing, per_lane, arrived
        )
        rim_rows = section_rims(sent)
        incoming = jnp.stack([rim_rows[2], rim_rows[0]])
        return (incoming, gskip_buf, glow_buf)

    backward_out = lax.fori_loop(
        0, tick_count, backward_tick, (empty_rows, empty_slots, empty_slots)
    )
    glow_buf = backward_out[2]
    grads_rows = lax.all_to_all(glow_buf, "dp", split_axis=2, concat_axis=3, tiled=True)
    acts_cells = lax.all_gather(acts_buf, "dp", axis=3, tiled=True)
    lane_grads = []
    for lane_index in range(lane_count):
        total = weight_grad_from_grads(
            acts_cells[lane_index, 0], grads_rows[lane_index, 0], FRAMES, HEIGHT, WIDTH
        )
        lane_grads.append(total)
    own_grads = lane_grads[0] + mirror_grads(lane_grads[1])
    return own_grads[None]


def solution(mesh):
    placed = (
        P(None, "chan", "dp"),
        P("section", ("chan", "dp"), None, None),
        P(None, "chan", "dp"),
    )
    return jax.shard_map(
        on_device,
        mesh=mesh,
        in_specs=placed,
        out_specs=P("section", ("chan", "dp"), None, None),
        check_vma=False,
    )
```

profile of v0, /device:TPU:8, one launch (start us, length us, event | category | flops | bytes accessed | tf_op | source)
XLA Modules:
  0.0 1673.4 jit_solution(5137266346502927320)
XLA Ops:
  6.5 15.7 collective-permute-start.10
  62.8 129.0 %all-gather.3.cloned.1.call-done = bf16[2,128,27,512]{3,0,2,1:T(2,128)(2,1)} async-done(((bf16[2,8,27,512]{3,0,2,1:T(2,128)(2,1)}), bf16[2,128,27,512]{3,0,2,1:T(2,128)(2,1)}) %all-gather.3.cloned.1.call-update) | async-done | bytes 7077904 | tf_op jit(solution)/shard_map/all_gather | solution.py:214
  191.8 15.5 fusion.311
  207.2 14.8 copy.1660
  226.2 14.8 copy.1661
  245.3 529.0 %while.42 = (s32[]{:T(128)}, bf16[2,128,128]{1,2,0:T(8,128)(2,1)S(1)}, bf16[2,1,128,128]{2,3,1,0:T(8,128)(2,1)S(1)}, bf16[2,1,128,128]{2,3,1,0:T(8,128)(2,1)S(1)...) while((s32[]{:T(128)}, ...), condition=%wide.region_4.5_spmd, body=%wide.region_0.4_spmd.sunk | while | flops 455368896 | bytes 31049684 | solution.py:266
  253.3 11.5 all_gather.20
  264.8 7.4 collective-permute-start
  280.1 8.2 collective-permute-start.2
  294.6 7.7 collective-permute-start.3
  321.0 10.7 all_gather.20
  331.7 9.2 collective-permute-start
  350.9 10.5 collective-permute-done.2
  384.3 10.8 all_gather.20
  403.4 11.6 collective-permute-start.1
  419.8 10.5 collective-permute-done.2
  451.3 10.7 all_gather.20
  467.7 8.9 collective-permute-start.1
  477.3 11.3 collective-permute-start.2
  515.1 10.8 all_gather.20
  525.9 10.2 collective-permute-start
  543.1 13.5 collective-permute-start.2
  564.3 8.3 collective-permute-start.4
  582.4 10.7 all_gather.20
  603.9 9.1 collective-permute-start.1
  619.2 9.0 collective-permute-done.2
  649.3 11.1 all_gather.20
  660.4 13.2 collective-permute-start
  676.3 7.7 collective-permute-start.2
  713.3 10.7 all_gather.20
  724.0 12.4 collective-permute-start
  739.3 13.3 collective-permute-start.2
  754.5 9.0 collective-permute-start.3
  775.6 744.8 %while.43 = (s32[]{:T(128)}, bf16[2,128,128]{1,2,0:T(8,128)(2,1)S(1)}, bf16[2,1,128,128]{2,3,1,0:T(8,128)(2,1)}, bf16[2,1,128,128]{2,3,1,0:T(8,128)(2,1)}, s32[2...) while((s32[]{:T(128)}, ...), condition=%wide.region_10.11_spmd, body=%wide.region_5.10_spmd.sunk | while | flops 454528576 | bytes 34589428 | solution.py:319
  787.0 36.6 %reduce-scatter.6.cloned.1.call-done = bf16[128,128]{1,0:T(8,128)(2,1)} async-done(((bf16[512,128]{1,0:T(8,128)(2,1)}), bf16[128,128]{1,0:T(8,128)(2,1)}) %reduce-scatter.6.cloned.1.call-update) | async-done | bytes 32784 | tf_op jit(solution)/shard_map/while
  825.3 12.8 collective-permute-start.7
  840.9 13.5 collective-permute-start.6
  881.8 35.2 %reduce-scatter.6.cloned.1.call-done = bf16[128,128]{1,0:T(8,128)(2,1)} async-done(((bf16[512,128]{1,0:T(8,128)(2,1)}), bf16[128,128]{1,0:T(8,128)(2,1)}) %reduce-scatter.6.cloned.1.call-update) | async-done | bytes 32784 | tf_op jit(solution)/shard_map/while
  918.6 12.8 collective-permute-start.7
  934.2 13.5 collective-permute-start.6
  973.5 17.4 %conditional.5 = (bf16[512,128]{0,1:T(8,128)(2,1)S(1)}) conditional(s32[]{:T(128)} %clamp.25, () %tuple.419, (bf16[128,128]{0,1:T(8,128)(2,1)S(1)}, bf16[3,128,4608]{2,1,0:T(8,128)(2,1)}) %tuple.420, (bf16[128,128]{0,1:T(8,128)(2,1)S(1)}, bf16[3,128,4608]{2,1,0:T(8,128)(2,1)}) %tuple.421), branch_computations={%region_6.6_spmd, %region_7.7_spmd, %region_8.8_spmd} | conditional | flops 453791232 | bytes 30786196 | solution.py:300
  992.4 17.1 %reduce-scatter.6.cloned.1.call-done = bf16[128,128]{1,0:T(8,128)(2,1)} async-done(((bf16[512,128]{1,0:T(8,128)(2,1)}), bf16[128,128]{1,0:T(8,128)(2,1)}) %reduce-scatter.6.cloned.1.call-update) | async-done | bytes 32784 | tf_op jit(solution)/shard_map/while
  1011.2 12.8 collective-permute-start.7
  1026.8 13.5 collective-permute-start.6
  1067.6 35.2 %reduce-scatter.6.cloned.1.call-done = bf16[128,128]{1,0:T(8,128)(2,1)} async-done(((bf16[512,128]{1,0:T(8,128)(2,1)}), bf16[128,128]{1,0:T(8,128)(2,1)}) %reduce-scatter.6.cloned.1.call-update) | async-done | bytes 32784 | tf_op jit(solution)/shard_map/while
  1104.6 12.8 collective-permute-start.7
  1120.2 13.5 collective-permute-start.6
  1161.0 35.2 %reduce-scatter.6.cloned.1.call-done = bf16[128,128]{1,0:T(8,128)(2,1)} async-done(((bf16[512,128]{1,0:T(8,128)(2,1)}), bf16[128,128]{1,0:T(8,128)(2,1)}) %reduce-scatter.6.cloned.1.call-update) | async-done | bytes 32784 | tf_op jit(solution)/shard_map/while
  1197.9 12.8 collective-permute-start.7
  1213.5 13.5 collective-permute-start.6
  1252.8 17.4 %conditional.5 = (bf16[512,128]{0,1:T(8,128)(2,1)S(1)}) conditional(s32[]{:T(128)} %clamp.25, () %tuple.419, (bf16[128,128]{0,1:T(8,128)(2,1)S(1)}, bf16[3,128,4608]{2,1,0:T(8,128)(2,1)}) %tuple.420, (bf16[128,128]{0,1:T(8,128)(2,1)S(1)}, bf16[3,128,4608]{2,1,0:T(8,128)(2,1)}) %tuple.421), branch_computations={%region_6.6_spmd, %region_7.7_spmd, %region_8.8_spmd} | conditional | flops 453791232 | bytes 30786196 | solution.py:300
  1271.7 17.0 %reduce-scatter.6.cloned.1.call-done = bf16[128,128]{1,0:T(8,128)(2,1)} async-done(((bf16[512,128]{1,0:T(8,128)(2,1)}), bf16[128,128]{1,0:T(8,128)(2,1)}) %reduce-scatter.6.cloned.1.call-update) | async-done | bytes 32784 | tf_op jit(solution)/shard_map/while
  1290.5 12.8 collective-permute-start.7
  1306.1 13.5 collective-permute-start.6
  1346.9 35.2 %reduce-scatter.6.cloned.1.call-done = bf16[128,128]{1,0:T(8,128)(2,1)} async-done(((bf16[512,128]{1,0:T(8,128)(2,1)}), bf16[128,128]{1,0:T(8,128)(2,1)}) %reduce-scatter.6.cloned.1.call-update) | async-done | bytes 32784 | tf_op jit(solution)/shard_map/while
  1383.7 12.8 collective-permute-start.7
  1399.4 13.5 collective-permute-start.6
  1440.2 33.5 %reduce-scatter.6.cloned.1.call-done = bf16[128,128]{1,0:T(8,128)(2,1)} async-done(((bf16[512,128]{1,0:T(8,128)(2,1)}), bf16[128,128]{1,0:T(8,128)(2,1)}) %reduce-scatter.6.cloned.1.call-update) | async-done | bytes 32784 | tf_op jit(solution)/shard_map/while
  1475.4 12.8 collective-permute-start.7
  1491.0 13.5 collective-permute-start.6
  1526.6 10.6 all-to-all-done
  1557.2 66.0 %all-gather.5.cloned.1.call-done = bf16[2,1,512,2048]{2,3,1,0:T(8,128)(2,1)} async-done(((bf16[2,1,512,128]{2,3,1,0:T(8,128)(2,1)}), bf16[2,1,512,2048]{2,3,1,0:T(8,128)(2,1)}) %all-gather.5.cloned.1.call-update) | async-done | bytes 4194320 | tf_op jit(solution)/shard_map/all_gather | solution.py:324
  1628.0 7.6 collective-permute-start.13
  1636.1 10.5 collective-permute-done.13
  (906 shorter events, 526.8 us)
Async XLA Ops:
  6.5 185.2 %all-gather.3.cloned.1.call-start = ((), (), s32[]{:S(2)}) async-start(), calls=%async_computation.2 | async-start | bytes 7520256 | tf_op jit(solution)/shard_map/all_gather | solution.py:214
  6.5 21.6 %collective-permute-start.10 = (bf16[8,27,512]{2,0,1:T(8,128)(2,1)}, bf16[8,27,512]{2,0,1:T(8,128)(2,1)S(1)}, u32[]{:S(2)}, u32[]{:S(2)}) collective-permute-start(bf16[8,27,512]{2,0,1:T(8,128)(2,1)} %bitcast.642), channel_id=1, source_target_pairs={{0,64},{64,0},{128,192},{192,128},{256,320},{320,256},{384,448},{4... | collective-permute-start | bytes 663560 | tf_op jit(solution)/shard_map/ppermute | solution.py:19
  264.8 42.8 %collective-permute-start = (bf16[1,128,128]{1,2,0:T(8,128)(2,1)S(1)}, bf16[1,128,128]{1,2,0:T(8,128)(2,1)S(1)}, u32[]{:S(2)}, u32[]{:S(2)}) collective-permute-start(bf16[1,128,128]{1,2,0:T(8,128)(2,1)S(1)} %fusion.351), channel_id=1, source_target_pairs={{64,0},{128,64},{192,128},{256,192},{320,256},{384,320},{448,384},... | collective-permute-start | bytes 98312 | tf_op jit(solution)/shard_map/while/body/eval_jaxpr/ppermute | solution.py:30
  272.2 35.5 %collective-permute-start.1 = (bf16[1,128,128]{1,2,0:T(8,128)(2,1)S(1)}, bf16[1,128,128]{1,2,0:T(8,128)(2,1)S(1)}, u32[]{:S(2)}, u32[]{:S(2)}) collective-permute-start(bf16[1,128,128]{1,2,0:T(8,128)(2,1)S(1)} %fusion.351), channel_id=1, source_target_pairs={{0,64},{64,128},{128,192},{192,256},{256,320},{320,384},{384,448},... | collective-permute-start | bytes 98312 | tf_op jit(solution)/shard_map/while/body/eval_jaxpr/ppermute | solution.py:29
  280.1 14.5 collective-permute-start.2
  294.6 11.1 collective-permute-start.3
  331.7 42.8 %collective-permute-start = (bf16[1,128,128]{1,2,0:T(8,128)(2,1)S(1)}, bf16[1,128,128]{1,2,0:T(8,128)(2,1)S(1)}, u32[]{:S(2)}, u32[]{:S(2)}) collective-permute-start(bf16[1,128,128]{1,2,0:T(8,128)(2,1)S(1)} %fusion.351), channel_id=1, source_target_pairs={{64,0},{128,64},{192,128},{256,192},{320,256},{384,320},{448,384},... | collective-permute-start | bytes 98312 | tf_op jit(solution)/shard_map/while/body/eval_jaxpr/ppermute | solution.py:30
  340.9 33.7 %collective-permute-start.1 = (bf16[1,128,128]{1,2,0:T(8,128)(2,1)S(1)}, bf16[1,128,128]{1,2,0:T(8,128)(2,1)S(1)}, u32[]{:S(2)}, u32[]{:S(2)}) collective-permute-start(bf16[1,128,128]{1,2,0:T(8,128)(2,1)S(1)} %fusion.351), channel_id=1, source_target_pairs={{0,64},{64,128},{128,192},{192,256},{256,320},{320,384},{384,448},... | collective-permute-start | bytes 98312 | tf_op jit(solution)/shard_map/while/body/eval_jaxpr/ppermute | solution.py:29
  347.0 14.5 collective-permute-start.2
  400.5 37.5 %collective-permute-start = (bf16[1,128,128]{1,2,0:T(8,128)(2,1)S(1)}, bf16[1,128,128]{1,2,0:T(8,128)(2,1)S(1)}, u32[]{:S(2)}, u32[]{:S(2)}) collective-permute-start(bf16[1,128,128]{1,2,0:T(8,128)(2,1)S(1)} %fusion.351), channel_id=1, source_target_pairs={{64,0},{128,64},{192,128},{256,192},{320,256},{384,320},{448,384},... | collective-permute-start | bytes 98312 | tf_op jit(solution)/shard_map/while/body/eval_jaxpr/ppermute | solution.py:30
  403.4 34.6 %collective-permute-start.1 = (bf16[1,128,128]{1,2,0:T(8,128)(2,1)S(1)}, bf16[1,128,128]{1,2,0:T(8,128)(2,1)S(1)}, u32[]{:S(2)}, u32[]{:S(2)}) collective-permute-start(bf16[1,128,128]{1,2,0:T(8,128)(2,1)S(1)} %fusion.351), channel_id=1, source_target_pairs={{0,64},{64,128},{128,192},{192,256},{256,320},{320,384},{384,448},... | collective-permute-start | bytes 98312 | tf_op jit(solution)/shard_map/while/body/eval_jaxpr/ppermute | solution.py:29
  415.8 14.5 collective-permute-start.2
  462.0 43.3 %collective-permute-start = (bf16[1,128,128]{1,2,0:T(8,128)(2,1)S(1)}, bf16[1,128,128]{1,2,0:T(8,128)(2,1)S(1)}, u32[]{:S(2)}, u32[]{:S(2)}) collective-permute-start(bf16[1,128,128]{1,2,0:T(8,128)(2,1)S(1)} %fusion.351), channel_id=1, source_target_pairs={{64,0},{128,64},{192,128},{256,192},{320,256},{384,320},{448,384},... | collective-permute-start | bytes 98312 | tf_op jit(solution)/shard_map/while/body/eval_jaxpr/ppermute | solution.py:30
  467.7 37.6 %collective-permute-start.1 = (bf16[1,128,128]{1,2,0:T(8,128)(2,1)S(1)}, bf16[1,128,128]{1,2,0:T(8,128)(2,1)S(1)}, u32[]{:S(2)}, u32[]{:S(2)}) collective-permute-start(bf16[1,128,128]{1,2,0:T(8,128)(2,1)S(1)} %fusion.351), channel_id=1, source_target_pairs={{0,64},{64,128},{128,192},{192,256},{256,320},{320,384},{384,448},... | collective-permute-start | bytes 98312 | tf_op jit(solution)/shard_map/while/body/eval_jaxpr/ppermute | solution.py:29
  477.3 14.5 collective-permute-start.2
  525.9 46.7 %collective-permute-start = (bf16[1,128,128]{1,2,0:T(8,128)(2,1)S(1)}, bf16[1,128,128]{1,2,0:T(8,128)(2,1)S(1)}, u32[]{:S(2)}, u32[]{:S(2)}) collective-permute-start(bf16[1,128,128]{1,2,0:T(8,128)(2,1)S(1)} %fusion.351), channel_id=1, source_target_pairs={{64,0},{128,64},{192,128},{256,192},{320,256},{384,320},{448,384},... | collective-permute-start | bytes 98312 | tf_op jit(solution)/shard_map/while/body/eval_jaxpr/ppermute | solution.py:30
  536.1 36.6 %collective-permute-start.1 = (bf16[1,128,128]{1,2,0:T(8,128)(2,1)S(1)}, bf16[1,128,128]{1,2,0:T(8,128)(2,1)S(1)}, u32[]{:S(2)}, u32[]{:S(2)}) collective-permute-start(bf16[1,128,128]{1,2,0:T(8,128)(2,1)S(1)} %fusion.351), channel_id=1, source_target_pairs={{0,64},{64,128},{128,192},{192,256},{256,320},{320,384},{384,448},... | collective-permute-start | bytes 98312 | tf_op jit(solution)/shard_map/while/body/eval_jaxpr/ppermute | solution.py:29
  543.1 15.4 collective-permute-start.2
  564.3 10.2 collective-permute-start.4
  598.4 37.5 %collective-permute-start = (bf16[1,128,128]{1,2,0:T(8,128)(2,1)S(1)}, bf16[1,128,128]{1,2,0:T(8,128)(2,1)S(1)}, u32[]{:S(2)}, u32[]{:S(2)}) collective-permute-start(bf16[1,128,128]{1,2,0:T(8,128)(2,1)S(1)} %fusion.351), channel_id=1, source_target_pairs={{64,0},{128,64},{192,128},{256,192},{320,256},{384,320},{448,384},... | collective-permute-start | bytes 98312 | tf_op jit(solution)/shard_map/while/body/eval_jaxpr/ppermute | solution.py:30
  603.9 32.0 %collective-permute-start.1 = (bf16[1,128,128]{1,2,0:T(8,128)(2,1)S(1)}, bf16[1,128,128]{1,2,0:T(8,128)(2,1)S(1)}, u32[]{:S(2)}, u32[]{:S(2)}) collective-permute-start(bf16[1,128,128]{1,2,0:T(8,128)(2,1)S(1)} %fusion.351), channel_id=1, source_target_pairs={{0,64},{64,128},{128,192},{192,256},{256,320},{320,384},{384,448},... | collective-permute-start | bytes 98312 | tf_op jit(solution)/shard_map/while/body/eval_jaxpr/ppermute | solution.py:29
  613.7 14.5 collective-permute-start.2
  660.4 43.2 %collective-permute-start = (bf16[1,128,128]{1,2,0:T(8,128)(2,1)S(1)}, bf16[1,128,128]{1,2,0:T(8,128)(2,1)S(1)}, u32[]{:S(2)}, u32[]{:S(2)}) collective-permute-start(bf16[1,128,128]{1,2,0:T(8,128)(2,1)S(1)} %fusion.351), channel_id=1, source_target_pairs={{64,0},{128,64},{192,128},{256,192},{320,256},{384,320},{448,384},... | collective-permute-start | bytes 98312 | tf_op jit(solution)/shard_map/while/body/eval_jaxpr/ppermute | solution.py:30
  673.6 29.9 %collective-permute-start.1 = (bf16[1,128,128]{1,2,0:T(8,128)(2,1)S(1)}, bf16[1,128,128]{1,2,0:T(8,128)(2,1)S(1)}, u32[]{:S(2)}, u32[]{:S(2)}) collective-permute-start(bf16[1,128,128]{1,2,0:T(8,128)(2,1)S(1)} %fusion.351), channel_id=1, source_target_pairs={{0,64},{64,128},{128,192},{192,256},{256,320},{320,384},{384,448},... | collective-permute-start | bytes 98312 | tf_op jit(solution)/shard_map/while/body/eval_jaxpr/ppermute | solution.py:29
  676.3 14.6 collective-permute-start.2
  724.0 44.8 %collective-permute-start = (bf16[1,128,128]{1,2,0:T(8,128)(2,1)S(1)}, bf16[1,128,128]{1,2,0:T(8,128)(2,1)S(1)}, u32[]{:S(2)}, u32[]{:S(2)}) collective-permute-start(bf16[1,128,128]{1,2,0:T(8,128)(2,1)S(1)} %fusion.351), channel_id=1, source_target_pairs={{64,0},{128,64},{192,128},{256,192},{320,256},{384,320},{448,384},... | collective-permute-start | bytes 98312 | tf_op jit(solution)/shard_map/while/body/eval_jaxpr/ppermute | solution.py:30
  736.4 32.4 %collective-permute-start.1 = (bf16[1,128,128]{1,2,0:T(8,128)(2,1)S(1)}, bf16[1,128,128]{1,2,0:T(8,128)(2,1)S(1)}, u32[]{:S(2)}, u32[]{:S(2)}) collective-permute-start(bf16[1,128,128]{1,2,0:T(8,128)(2,1)S(1)} %fusion.351), channel_id=1, source_target_pairs={{0,64},{64,128},{128,192},{192,256},{256,320},{320,384},{384,448},... | collective-permute-start | bytes 98312 | tf_op jit(solution)/shard_map/while/body/eval_jaxpr/ppermute | solution.py:29
  739.3 15.2 collective-permute-start.2
  754.5 12.4 collective-permute-start.3
  775.6 48.0 %reduce-scatter.6.cloned.1.call-start = ((), (), s32[]{:S(2)}) async-start(), calls=%async_computation.4 | async-start | bytes 163840 | tf_op jit(solution)/shard_map/while
  825.3 29.2 %collective-permute-start.7 = (bf16[128,128]{0,1:T(8,128)(2,1)S(1)}, bf16[128,128]{0,1:T(8,128)(2,1)S(1)}, u32[]{:S(2)}, u32[]{:S(2)}) collective-permute-start(bf16[128,128]{0,1:T(8,128)(2,1)S(1)} %convert_select_fusion.2), channel_id=1, source_target_pairs={{0,64},{64,0},{128,192},{192,128},{256,320},{320,256},{384,448},{4... | collective-permute-start | bytes 98312 | tf_op jit(solution)/shard_map/while/body/eval_jaxpr/ppermute | solution.py:19
  839.0 25.5 %collective-permute-start.5 = (bf16[1,128,128]{1,2,0:T(8,128)(2,1)S(1)}, bf16[1,128,128]{1,2,0:T(8,128)(2,1)S(1)}, u32[]{:S(2)}, u32[]{:S(2)}) collective-permute-start(bf16[1,128,128]{1,2,0:T(8,128)(2,1)S(1)} %fusion.357), channel_id=1, source_target_pairs={{0,64},{64,128},{128,192},{192,256},{256,320},{320,384},{384,448},... | collective-permute-start | bytes 98312 | tf_op jit(solution)/shard_map/while/body/eval_jaxpr/ppermute | solution.py:29
  840.9 23.6 %collective-permute-start.6 = (bf16[1,128,128]{1,2,0:T(8,128)(2,1)S(1)}, bf16[1,128,128]{1,2,0:T(8,128)(2,1)S(1)}, u32[]{:S(2)}, u32[]{:S(2)}) collective-permute-start(bf16[1,128,128]{1,2,0:T(8,128)(2,1)S(1)} %fusion.357), channel_id=1, source_target_pairs={{64,0},{128,64},{192,128},{256,192},{320,256},{384,320},{448,384},... | collective-permute-start | bytes 98312 | tf_op jit(solution)/shard_map/while/body/eval_jaxpr/ppermute | solution.py:30
  870.3 46.6 %reduce-scatter.6.cloned.1.call-start = ((), (), s32[]{:S(2)}) async-start(), calls=%async_computation.4 | async-start | bytes 163840 | tf_op jit(solution)/shard_map/while
  918.6 29.2 %collective-permute-start.7 = (bf16[128,128]{0,1:T(8,128)(2,1)S(1)}, bf16[128,128]{0,1:T(8,128)(2,1)S(1)}, u32[]{:S(2)}, u32[]{:S(2)}) collective-permute-start(bf16[128,128]{0,1:T(8,128)(2,1)S(1)} %convert_select_fusion.2), channel_id=1, source_target_pairs={{0,64},{64,0},{128,192},{192,128},{256,320},{320,256},{384,448},{4... | collective-permute-start | bytes 98312 | tf_op jit(solution)/shard_map/while/body/eval_jaxpr/ppermute | solution.py:19
  932.3 25.6 %collective-permute-start.5 = (bf16[1,128,128]{1,2,0:T(8,128)(2,1)S(1)}, bf16[1,128,128]{1,2,0:T(8,128)(2,1)S(1)}, u32[]{:S(2)}, u32[]{:S(2)}) collective-permute-start(bf16[1,128,128]{1,2,0:T(8,128)(2,1)S(1)} %fusion.357), channel_id=1, source_target_pairs={{0,64},{64,128},{128,192},{192,256},{256,320},{320,384},{384,448},... | collective-permute-start | bytes 98312 | tf_op jit(solution)/shard_map/while/body/eval_jaxpr/ppermute | solution.py:29
  934.2 23.7 %collective-permute-start.6 = (bf16[1,128,128]{1,2,0:T(8,128)(2,1)S(1)}, bf16[1,128,128]{1,2,0:T(8,128)(2,1)S(1)}, u32[]{:S(2)}, u32[]{:S(2)}) collective-permute-start(bf16[1,128,128]{1,2,0:T(8,128)(2,1)S(1)} %fusion.357), channel_id=1, source_target_pairs={{64,0},{128,64},{192,128},{256,192},{320,256},{384,320},{448,384},... | collective-permute-start | bytes 98312 | tf_op jit(solution)/shard_map/while/body/eval_jaxpr/ppermute | solution.py:30
  963.6 45.8 %reduce-scatter.6.cloned.1.call-start = ((), (), s32[]{:S(2)}) async-start(), calls=%async_computation.4 | async-start | bytes 163840 | tf_op jit(solution)/shard_map/while
  1011.2 29.2 %collective-permute-start.7 = (bf16[128,128]{0,1:T(8,128)(2,1)S(1)}, bf16[128,128]{0,1:T(8,128)(2,1)S(1)}, u32[]{:S(2)}, u32[]{:S(2)}) collective-permute-start(bf16[128,128]{0,1:T(8,128)(2,1)S(1)} %convert_select_fusion.2), channel_id=1, source_target_pairs={{0,64},{64,0},{128,192},{192,128},{256,320},{320,256},{384,448},{4... | collective-permute-start | bytes 98312 | tf_op jit(solution)/shard_map/while/body/eval_jaxpr/ppermute | solution.py:19
  1024.9 25.5 %collective-permute-start.5 = (bf16[1,128,128]{1,2,0:T(8,128)(2,1)S(1)}, bf16[1,128,128]{1,2,0:T(8,128)(2,1)S(1)}, u32[]{:S(2)}, u32[]{:S(2)}) collective-permute-start(bf16[1,128,128]{1,2,0:T(8,128)(2,1)S(1)} %fusion.357), channel_id=1, source_target_pairs={{0,64},{64,128},{128,192},{192,256},{256,320},{320,384},{384,448},... | collective-permute-start | bytes 98312 | tf_op jit(solution)/shard_map/while/body/eval_jaxpr/ppermute | solution.py:29
  1026.8 23.6 %collective-permute-start.6 = (bf16[1,128,128]{1,2,0:T(8,128)(2,1)S(1)}, bf16[1,128,128]{1,2,0:T(8,128)(2,1)S(1)}, u32[]{:S(2)}, u32[]{:S(2)}) collective-permute-start(bf16[1,128,128]{1,2,0:T(8,128)(2,1)S(1)} %fusion.357), channel_id=1, source_target_pairs={{64,0},{128,64},{192,128},{256,192},{320,256},{384,320},{448,384},... | collective-permute-start | bytes 98312 | tf_op jit(solution)/shard_map/while/body/eval_jaxpr/ppermute | solution.py:30
  1056.2 46.7 %reduce-scatter.6.cloned.1.call-start = ((), (), s32[]{:S(2)}) async-start(), calls=%async_computation.4 | async-start | bytes 163840 | tf_op jit(solution)/shard_map/while
  1104.6 29.2 %collective-permute-start.7 = (bf16[128,128]{0,1:T(8,128)(2,1)S(1)}, bf16[128,128]{0,1:T(8,128)(2,1)S(1)}, u32[]{:S(2)}, u32[]{:S(2)}) collective-permute-start(bf16[128,128]{0,1:T(8,128)(2,1)S(1)} %convert_select_fusion.2), channel_id=1, source_target_pairs={{0,64},{64,0},{128,192},{192,128},{256,320},{320,256},{384,448},{4... | collective-permute-start | bytes 98312 | tf_op jit(solution)/shard_map/while/body/eval_jaxpr/ppermute | solution.py:19
  1118.3 25.6 %collective-permute-start.5 = (bf16[1,128,128]{1,2,0:T(8,128)(2,1)S(1)}, bf16[1,128,128]{1,2,0:T(8,128)(2,1)S(1)}, u32[]{:S(2)}, u32[]{:S(2)}) collective-permute-start(bf16[1,128,128]{1,2,0:T(8,128)(2,1)S(1)} %fusion.357), channel_id=1, source_target_pairs={{0,64},{64,128},{128,192},{192,256},{256,320},{320,384},{384,448},... | collective-permute-start | bytes 98312 | tf_op jit(solution)/shard_map/while/body/eval_jaxpr/ppermute | solution.py:29
  1120.2 23.6 %collective-permute-start.6 = (bf16[1,128,128]{1,2,0:T(8,128)(2,1)S(1)}, bf16[1,128,128]{1,2,0:T(8,128)(2,1)S(1)}, u32[]{:S(2)}, u32[]{:S(2)}) collective-permute-start(bf16[1,128,128]{1,2,0:T(8,128)(2,1)S(1)} %fusion.357), channel_id=1, source_target_pairs={{64,0},{128,64},{192,128},{256,192},{320,256},{384,320},{448,384},... | collective-permute-start | bytes 98312 | tf_op jit(solution)/shard_map/while/body/eval_jaxpr/ppermute | solution.py:30
  1149.6 46.6 %reduce-scatter.6.cloned.1.call-start = ((), (), s32[]{:S(2)}) async-start(), calls=%async_computation.4 | async-start | bytes 163840 | tf_op jit(solution)/shard_map/while
  1197.9 29.2 %collective-permute-start.7 = (bf16[128,128]{0,1:T(8,128)(2,1)S(1)}, bf16[128,128]{0,1:T(8,128)(2,1)S(1)}, u32[]{:S(2)}, u32[]{:S(2)}) collective-permute-start(bf16[128,128]{0,1:T(8,128)(2,1)S(1)} %convert_select_fusion.2), channel_id=1, source_target_pairs={{0,64},{64,0},{128,192},{192,128},{256,320},{320,256},{384,448},{4... | collective-permute-start | bytes 98312 | tf_op jit(solution)/shard_map/while/body/eval_jaxpr/ppermute | solution.py:19
  1211.6 25.5 %collective-permute-start.5 = (bf16[1,128,128]{1,2,0:T(8,128)(2,1)S(1)}, bf16[1,128,128]{1,2,0:T(8,128)(2,1)S(1)}, u32[]{:S(2)}, u32[]{:S(2)}) collective-permute-start(bf16[1,128,128]{1,2,0:T(8,128)(2,1)S(1)} %fusion.357), channel_id=1, source_target_pairs={{0,64},{64,128},{128,192},{192,256},{256,320},{320,384},{384,448},... | collective-permute-start | bytes 98312 | tf_op jit(solution)/shard_map/while/body/eval_jaxpr/ppermute | solution.py:29
  1213.5 23.6 %collective-permute-start.6 = (bf16[1,128,128]{1,2,0:T(8,128)(2,1)S(1)}, bf16[1,128,128]{1,2,0:T(8,128)(2,1)S(1)}, u32[]{:S(2)}, u32[]{:S(2)}) collective-permute-start(bf16[1,128,128]{1,2,0:T(8,128)(2,1)S(1)} %fusion.357), channel_id=1, source_target_pairs={{64,0},{128,64},{192,128},{256,192},{320,256},{384,320},{448,384},... | collective-permute-start | bytes 98312 | tf_op jit(solution)/shard_map/while/body/eval_jaxpr/ppermute | solution.py:30
  1243.0 45.8 %reduce-scatter.6.cloned.1.call-start = ((), (), s32[]{:S(2)}) async-start(), calls=%async_computation.4 | async-start | bytes 163840 | tf_op jit(solution)/shard_map/while
  1290.5 29.2 %collective-permute-start.7 = (bf16[128,128]{0,1:T(8,128)(2,1)S(1)}, bf16[128,128]{0,1:T(8,128)(2,1)S(1)}, u32[]{:S(2)}, u32[]{:S(2)}) collective-permute-start(bf16[128,128]{0,1:T(8,128)(2,1)S(1)} %convert_select_fusion.2), channel_id=1, source_target_pairs={{0,64},{64,0},{128,192},{192,128},{256,320},{320,256},{384,448},{4... | collective-permute-start | bytes 98312 | tf_op jit(solution)/shard_map/while/body/eval_jaxpr/ppermute | solution.py:19
  1304.2 25.5 %collective-permute-start.5 = (bf16[1,128,128]{1,2,0:T(8,128)(2,1)S(1)}, bf16[1,128,128]{1,2,0:T(8,128)(2,1)S(1)}, u32[]{:S(2)}, u32[]{:S(2)}) collective-permute-start(bf16[1,128,128]{1,2,0:T(8,128)(2,1)S(1)} %fusion.357), channel_id=1, source_target_pairs={{0,64},{64,128},{128,192},{192,256},{256,320},{320,384},{384,448},... | collective-permute-start | bytes 98312 | tf_op jit(solution)/shard_map/while/body/eval_jaxpr/ppermute | solution.py:29
  1306.1 23.6 %collective-permute-start.6 = (bf16[1,128,128]{1,2,0:T(8,128)(2,1)S(1)}, bf16[1,128,128]{1,2,0:T(8,128)(2,1)S(1)}, u32[]{:S(2)}, u32[]{:S(2)}) collective-permute-start(bf16[1,128,128]{1,2,0:T(8,128)(2,1)S(1)} %fusion.357), channel_id=1, source_target_pairs={{64,0},{128,64},{192,128},{256,192},{320,256},{384,320},{448,384},... | collective-permute-start | bytes 98312 | tf_op jit(solution)/shard_map/while/body/eval_jaxpr/ppermute | solution.py:30
  1335.5 46.6 %reduce-scatter.6.cloned.1.call-start = ((), (), s32[]{:S(2)}) async-start(), calls=%async_computation.4 | async-start | bytes 163840 | tf_op jit(solution)/shard_map/while
  1383.7 29.2 %collective-permute-start.7 = (bf16[128,128]{0,1:T(8,128)(2,1)S(1)}, bf16[128,128]{0,1:T(8,128)(2,1)S(1)}, u32[]{:S(2)}, u32[]{:S(2)}) collective-permute-start(bf16[128,128]{0,1:T(8,128)(2,1)S(1)} %convert_select_fusion.2), channel_id=1, source_target_pairs={{0,64},{64,0},{128,192},{192,128},{256,320},{320,256},{384,448},{4... | collective-permute-start | bytes 98312 | tf_op jit(solution)/shard_map/while/body/eval_jaxpr/ppermute | solution.py:19
  1397.4 25.6 %collective-permute-start.5 = (bf16[1,128,128]{1,2,0:T(8,128)(2,1)S(1)}, bf16[1,128,128]{1,2,0:T(8,128)(2,1)S(1)}, u32[]{:S(2)}, u32[]{:S(2)}) collective-permute-start(bf16[1,128,128]{1,2,0:T(8,128)(2,1)S(1)} %fusion.357), channel_id=1, source_target_pairs={{0,64},{64,128},{128,192},{192,256},{256,320},{320,384},{384,448},... | collective-permute-start | bytes 98312 | tf_op jit(solution)/shard_map/while/body/eval_jaxpr/ppermute | solution.py:29
  1399.4 23.6 %collective-permute-start.6 = (bf16[1,128,128]{1,2,0:T(8,128)(2,1)S(1)}, bf16[1,128,128]{1,2,0:T(8,128)(2,1)S(1)}, u32[]{:S(2)}, u32[]{:S(2)}) collective-permute-start(bf16[1,128,128]{1,2,0:T(8,128)(2,1)S(1)} %fusion.357), channel_id=1, source_target_pairs={{64,0},{128,64},{192,128},{256,192},{320,256},{384,320},{448,384},... | collective-permute-start | bytes 98312 | tf_op jit(solution)/shard_map/while/body/eval_jaxpr/ppermute | solution.py:30
  1428.8 44.9 %reduce-scatter.6.cloned.1.call-start = ((), (), s32[]{:S(2)}) async-start(), calls=%async_computation.4 | async-start | bytes 163840 | tf_op jit(solution)/shard_map/while
  1475.4 29.2 %collective-permute-start.7 = (bf16[128,128]{0,1:T(8,128)(2,1)S(1)}, bf16[128,128]{0,1:T(8,128)(2,1)S(1)}, u32[]{:S(2)}, u32[]{:S(2)}) collective-permute-start(bf16[128,128]{0,1:T(8,128)(2,1)S(1)} %convert_select_fusion.2), channel_id=1, source_target_pairs={{0,64},{64,0},{128,192},{192,128},{256,320},{320,256},{384,448},{4... | collective-permute-start | bytes 98312 | tf_op jit(solution)/shard_map/while/body/eval_jaxpr/ppermute | solution.py:19
  1489.1 25.5 %collective-permute-start.5 = (bf16[1,128,128]{1,2,0:T(8,128)(2,1)S(1)}, bf16[1,128,128]{1,2,0:T(8,128)(2,1)S(1)}, u32[]{:S(2)}, u32[]{:S(2)}) collective-permute-start(bf16[1,128,128]{1,2,0:T(8,128)(2,1)S(1)} %fusion.357), channel_id=1, source_target_pairs={{0,64},{64,128},{128,192},{192,256},{256,320},{320,384},{384,448},... | collective-permute-start | bytes 98312 | tf_op jit(solution)/shard_map/while/body/eval_jaxpr/ppermute | solution.py:29
  1491.0 23.6 %collective-permute-start.6 = (bf16[1,128,128]{1,2,0:T(8,128)(2,1)S(1)}, bf16[1,128,128]{1,2,0:T(8,128)(2,1)S(1)}, u32[]{:S(2)}, u32[]{:S(2)}) collective-permute-start(bf16[1,128,128]{1,2,0:T(8,128)(2,1)S(1)} %fusion.357), channel_id=1, source_target_pairs={{64,0},{128,64},{192,128},{256,192},{320,256},{384,320},{448,384},... | collective-permute-start | bytes 98312 | tf_op jit(solution)/shard_map/while/body/eval_jaxpr/ppermute | solution.py:30
  1520.4 102.8 %all-gather.5.cloned.1.call-start = ((), (), s32[]{:S(2)}) async-start(), calls=%async_computation.3 | async-start | bytes 4456448 | tf_op jit(solution)/shard_map/all_gather | solution.py:324
  1522.8 14.4 all-to-all-start
  1628.0 18.6 %collective-permute-start.13 = (bf16[8,27,512]{2,1,0:T(8,128)(2,1)S(1)}, bf16[8,27,512]{2,1,0:T(8,128)(2,1)S(1)}, u32[]{:S(2)}, u32[]{:S(2)}) collective-permute-start(bf16[8,27,512]{2,1,0:T(8,128)(2,1)S(1)} %pad_maximum_fusion.3), channel_id=1, source_target_pairs={{0,64},{64,0},{128,192},{192,128},{256,320},{320,256},{384,448},{4... | collective-permute-start | bytes 663560 | tf_op jit(solution)/shard_map/ppermute | solution.py:19
  (87 other events, 1684.2 us)
Sparse Core Ops, SparseCore 0:
  62.8 128.8 all-gather.2
  786.4 37.1 reduce-scatter.5
  881.2 35.7 reduce-scatter.5
  991.8 17.6 reduce-scatter.5
  1067.1 35.7 reduce-scatter.5
  1160.4 35.7 reduce-scatter.5
  1271.2 17.5 reduce-scatter.5
  1346.3 35.7 reduce-scatter.5
  1439.6 33.9 reduce-scatter.5
  1523.0 100.1 all-gather.4
where the time goes:
time: 1680 us; the launch traced here: 1670 us
  waiting for transfers between devices  607 us (36%)
  starting transfers between devices  570 us (34%)
  local copies, waits for them, and re-layouts  177 us (11%)
  loops' own time  125 us (7%)
  blocking collectives  86.9 us (5%)
  other arithmetic  74.3 us (4%)
  matrix products  19 us (1%)
    ppermute x54, starting transfers between devices, from_partner(): return lax.ppermute(block, axis, route)  323 us
    while x16, waiting for transfers between devices  245 us
    ppermute x16, starting transfers between devices, with_halo(): after = lax.ppermute(first, axis, down)  175 us
    ppermute x54, waiting for transfers between devices, from_partner(): return lax.ppermute(block, axis, route)  156 us
    all_gather x1, waiting for transfers between devices, on_device(): lane_kernels = lax.all_gather(lane_shares, 'dp', axis=1, tiled=True)  129 us
    all_gather x8, blocking collectives, channel_gather(): return lax.all_gather(source, 'chan', axis=0, tiled=True)  86.9 us
    ppermute x16, starting transfers between devices, with_halo(): before = lax.ppermute(last, axis, up)  67.9 us
    another operation x1, loops' own time, on_device(): lax.fori_loop(0, tick_count, forward_tick, (empty_rows, empty_slots, empt...  67.6 us
  transfers between devices with their start and end apart: 97, of which 52 were waited for; matrix products, arithmetic and copies ran while one was open for 3% of the time, Pallas kernels for 0%

commit v1 on v0

v1 whole, which is shorter than its diff:
```python
import jax
import jax.numpy as jnp
from jax import lax
from jax.experimental import pallas as pl
from jax.experimental.pallas import tpu as pltpu
from jax.sharding import Mesh, PartitionSpec as P

F32 = jnp.float32
BF16 = jnp.bfloat16
LAYERS = 8
CELLS = 128
TAPS = [(df, dh, dw) for df in (-1, 0, 1) for dh in (-1, 0, 1) for dw in (-1, 0, 1)]
PLACE = [2 * l if l < 4 else 15 - 2 * l for l in range(LAYERS)]


def shifted(source, move):
    df, dh, dw = move
    if move == (0, 0, 0):
        return source
    lane = lax.broadcasted_iota(jnp.int32, (1, CELLS), 1)
    f, h, w = lane // 32 + df, (lane // 8) % 4 + dh, lane % 8 + dw
    inside = (f >= 0) & (f < 4) & (h >= 0) & (h < 4) & (w >= 0) & (w < 8)
    turned = pltpu.roll(source, (-(32 * df + 8 * dh + dw)) % CELLS, 1)
    return jnp.where(inside, turned, 0.0)


def forward_kernel(x_ref, skip_ref, w_ref, act_ref, out_ref):
    summed = x_ref[...].astype(F32) + skip_ref[...].astype(F32)
    act = (summed * jax.nn.sigmoid(summed)).astype(BF16)
    act_ref[...] = act
    act = act.astype(F32)
    total = None
    for first in range(0, 27, 3):
        stacked = jnp.concatenate(
            [shifted(act, TAPS[k]).astype(BF16) for k in range(first, first + 3)], axis=0
        )
        matrix = jnp.concatenate(
            [w_ref[:, k].reshape(512, 256) for k in range(first, first + 3)], axis=1
        )
        part = lax.dot_general(
            matrix, stacked, (((1,), (0,)), ((), ())), preferred_element_type=F32
        )
        total = part if total is None else total + part
    out_ref[...] = total


def backward_kernel(g_ref, up_ref, x_ref, skip_ref, w_ref, sent_ref, pre_ref, pad_ref):
    grads = g_ref[...].astype(F32).T
    column = lax.broadcasted_iota(jnp.int32, (CELLS, 1), 0) % 8
    pad_ref[...] = jnp.zeros(pad_ref.shape, F32)
    for slot, move in enumerate((1, 0, -1)):
        turned = grads
        if move:
            turned = pltpu.roll(grads, (-move) % CELLS, 0)
            turned = jnp.where((column + move >= 0) & (column + move < 8), turned, 0.0)
        pad_ref[slot, 1:5, 1:5] = turned.reshape(4, 4, 8, 512)
    total = None
    for k, (df, dh, dw) in enumerate(TAPS):
        window = pad_ref[dw + 1, 1 - df : 5 - df, 1 - dh : 5 - dh]
        part = lax.dot_general(
            window.reshape(CELLS, 512).astype(BF16),
            w_ref[:, k].reshape(512, 256),
            (((1,), (0,)), ((), ())),
            preferred_element_type=F32,
        )
        total = part if total is None else total + part
    summed = x_ref[...].astype(F32) + skip_ref[...].astype(F32)
    sig = jax.nn.sigmoid(summed)
    pre = total.T * (sig * (1.0 + summed * (1.0 - sig)))
    pre_ref[...] = pre.astype(BF16)
    sent_ref[...] = (up_ref[...] + pre).astype(BF16)


def weight_grad_kernel(g_ref, a_ref, out_ref):
    total = None
    for v in range(0, 32, 2):
        rows = []
        for u in (v, v + 1):
            grads = g_ref[u].astype(F32)
            rows.append(
                jnp.concatenate(
                    [shifted(grads, tuple(-m for m in move)).astype(BF16) for move in TAPS], axis=0
                )
            )
        left = jnp.concatenate(rows, axis=1)
        right = jnp.concatenate([a_ref[v], a_ref[v + 1]], axis=1)
        part = lax.dot_general(
            left, right, (((1,), (1,)), ((), ())), preferred_element_type=F32
        )
        total = part if total is None else total + part
    out_ref[...] = total.astype(BF16)


def own_half(array, core):
    half = array.shape[0] // 2
    return lax.dynamic_slice_in_dim(array, core * half, half, axis=0)


def volume_half(pair, core, x, mirrored):
    picked = [jnp.where(x % 2 == 0, pair[0], pair[1]), jnp.where(x % 2 == 0, pair[1], pair[0])]
    got = []
    for turn in range(2):
        route = []
        for z in range(8):
            for c in range(2):
                for at in range(4):
                    source = (z * 2 + c) * 4 + at
                    micro = at % 2 if turn == 0 else 1 - at % 2
                    target_z = 7 - z if mirrored else z
                    route.append((source, (target_z * 2 + at // 2) * 4 + 2 * micro + c))
        got.append(lax.ppermute(picked[turn], ("zl", "core", "x"), route))
    low = x // 2 == 0
    return jnp.concatenate(
        [jnp.where(low, got[0], got[1]), jnp.where(low, got[1], got[0])], axis=0
    )


def other_partial(partial, core):
    both = lax.all_gather(partial.astype(BF16), "core", axis=0, tiled=False)
    return own_half(jnp.where(core == 0, both[1], both[0]), core)


def on_device(clips, weights, cotangents):
    y, zh, core, x = (lax.axis_index(a) for a in ("y", "zh", "core", "x"))
    layer = jnp.where(zh == 0, y, 7 - y)
    section = ("y", "zh")

    own = lax.all_to_all(
        weights[0].transpose(1, 0, 2).reshape(27, 8, 2, 256), "core", split_axis=2, concat_axis=1
    ).reshape(27, 16, 256)
    own = lax.ppermute(own, section, [(l, PLACE[l]) for l in range(LAYERS)])
    kernel = lax.all_gather(own, "zl", axis=0, tiled=False)
    kernel = lax.all_gather(kernel, "x", axis=0, tiled=False).reshape(32, 27, 16, 256)

    x_hold = volume_half(clips, core, x, False)
    carried = volume_half(cotangents, core, x, True)

    tile = jax.ShapeDtypeStruct((256, CELLS), BF16)
    forward = pl.pallas_call(
        forward_kernel,
        out_shape=(tile, jax.ShapeDtypeStruct((512, CELLS), F32)),
        name="conv_forward",
    )
    backward = pl.pallas_call(
        backward_kernel,
        out_shape=(tile, tile),
        scratch_shapes=(pltpu.VMEM((3, 6, 6, 8, 512), F32),),
        name="conv_backward",
    )
    across = [(z, 15 - z) for z in range(8)]

    skip = jnp.zeros((256, CELLS), BF16)
    for l in range(LAYERS):
        act, partial = forward(x_hold, skip, kernel)
        if l == LAYERS - 1:
            break
        update = own_half(partial, core) + other_partial(partial, core).astype(F32)
        out = (x_hold.astype(F32) + update).astype(BF16)
        if l == 3:
            skip = lax.ppermute(out, ("zh", "zl"), across)
            x_hold = jnp.where(layer == 4, skip, x_hold)
        else:
            got = lax.ppermute(out, section, [(PLACE[l], PLACE[l + 1])])
            x_hold = jnp.where(layer == l + 1, got, x_hold)

    acts = lax.all_gather(act, "zl", axis=0, tiled=False)
    acts = lax.all_gather(acts, "x", axis=0, tiled=False).reshape(32, 256, CELLS)

    back = [(b, a) for a, b in across]
    upstream = carried.astype(F32)
    for l in reversed(range(LAYERS)):
        low = upstream.astype(BF16)
        grads = lax.all_gather(low, "core", axis=0, tiled=True)
        if l == 0:
            break
        sent, pre = backward(grads, upstream, x_hold, skip, kernel)
        if l == 4:
            both = lax.ppermute(jnp.stack([sent, pre]), ("zh", "zl"), back)
            gskip = both[1].astype(F32)
            upstream = jnp.where(layer < 4, gskip, upstream)
            upstream = jnp.where(layer == 3, both[0].astype(F32) + gskip, upstream)
        else:
            got = lax.ppermute(sent, section, [(PLACE[l], PLACE[l - 1])]).astype(F32)
            if l < 4:
                got = got + gskip
            upstream = jnp.where(layer == l - 1, got, upstream)

    rows = grads.reshape(4, 8, 16, CELLS)
    rows = lax.all_to_all(rows, "x", split_axis=0, concat_axis=0)
    rows = lax.all_to_all(rows, "zl", split_axis=1, concat_axis=1).reshape(32, 16, CELLS)
    total = pl.pallas_call(
        weight_grad_kernel,
        out_shape=jax.ShapeDtypeStruct((432, 256), BF16),
        name="weight_grad",
    )(rows, acts)
    total = lax.all_to_all(
        total.reshape(27, 2, 8, 256), "core", split_axis=1, concat_axis=1
    )
    total = lax.ppermute(total, section, [(PLACE[l], l) for l in range(LAYERS)])
    return total.transpose(2, 0, 1, 3).reshape(1, 8, 27, 512).astype(F32)


def solution(mesh):
    fine = Mesh(mesh.devices.reshape(4, 2, 8, 2, 4), ("y", "zh", "zl", "core", "x"))
    placed = (
        P(None, "x", ("zl", "core")),
        P(("y", "zh"), ("x", "zl", "core"), None, None),
        P(None, "x", ("zl", "core")),
    )
    return jax.shard_map(
        on_device,
        mesh=fine,
        in_specs=placed,
        out_specs=P(("y", "zh"), ("x", "zl", "core"), None, None),
        check_vma=False,
    )
```

time: 1680 us -> 535 us (0.32)
  the two profiles are of different devices: /device:TPU:8 before, /device:TPU:57 now
where the time goes in v1:
time: 535 us; the launch traced here: 533 us
  waiting for transfers between devices  224 us (42%)
  blocking collectives  126 us (24%)
  Pallas kernels  87.1 us (16%)
  starting transfers between devices  52.6 us (10%)
  other arithmetic  24.3 us (5%)
  between operations  13.7 us (3%)
  local copies, waits for them, and re-layouts  5.52 us (1%)
    all_gather x1, waiting for transfers between devices, on_device(): lax.all_gather(kernel, 'x', axis=0, tiled=False).reshape(32, 27, 16, 256)  71.2 us
    all_gather x1, waiting for transfers between devices, on_device(): kernel = lax.all_gather(own, 'zl', axis=0, tiled=False)  61.3 us
    pallas_call x8, Pallas kernels, on_device(): act, partial = forward(x_hold, skip, kernel)  47 us
    all_gather x1, blocking collectives, on_device(): acts = lax.all_gather(act, 'zl', axis=0, tiled=False)  46.8 us
    pallas_call x7, Pallas kernels, on_device(): sent, pre = backward(grads, upstream, x_hold, skip, kernel)  36.3 us
    ppermute x1, waiting for transfers between devices, on_device(): total = lax.ppermute(total, section, [(PLACE[l], l) for l in range(LAYERS)])  32.1 us
    all_gather x8, blocking collectives, on_device(): grads = lax.all_gather(low, 'core', axis=0, tiled=True)  24.5 us
    ppermute x4, starting transfers between devices, volume_half(): got.append(lax.ppermute(picked[turn], ('zl', 'core', 'x'), route))  23.6 us
  transfers between devices with their start and end apart: 23, of which 9 were waited for; matrix products, arithmetic and copies ran while one was open for 2% of the time, Pallas kernels for 8%

profile of v1, /device:TPU:57, one launch (start us, length us, event | category | flops | bytes accessed | tf_op | source)
XLA Modules:
  0.0 533.3 jit_solution(12578409501159897198)
XLA Ops:
  6.5 1.0 broadcast_in_dim_reshape.3
  7.6 4.2 all_to_all.30
  11.8 15.2 %collective-permute-start.4 = (bf16[27,16,256]{2,1,0:T(8,128)(2,1)S(1)}, bf16[27,16,256]{2,1,0:T(8,128)(2,1)S(1)}, u32[]{:S(2)}, u32[]{:S(2)}) collective-permute-start(bf16[27,16,256]{2,1,0:T(8,128)(2,1)S(1)} %bitcast.55), channel_id=1, source_target_pairs={{0,0},{64,128},{128,256},{192,384},{256,448},{320,320},{384,192},{... | collective-permute-start | bytes 663560 | tf_op jit(solution)/shard_map/ppermute | solution.py:131
  27.0 19.6 %collective-permute-done.4 = bf16[27,16,256]{2,1,0:T(8,128)(2,1)S(1)} collective-permute-done((bf16[27,16,256]{2,1,0:T(8,128)(2,1)S(1)}, bf16[27,16,256]{2,1,0:T(8,128)(2,1)S(1)}, u32[]{:S(2)}, u32[]{:S(2)}) %collective-permute-start.4) | collective-permute-done | bytes 221216 | tf_op jit(solution)/shard_map/ppermute | solution.py:131
  47.5 61.3 %all-gather.15.cloned.1.call-done = bf16[216,16,256]{2,1,0:T(8,128)(2,1)} async-done(((bf16[27,16,256]{2,1,0:T(8,128)(2,1)}), bf16[216,16,256]{2,1,0:T(8,128)(2,1)}) %all-gather.15.cloned.1.call-update) | async-done | bytes 1769488 | tf_op jit(solution)/shard_map/all_gather | solution.py:132
  108.9 7.9 %collective-permute-start.2 = (bf16[128,128]{1,0:T(8,128)(2,1)S(1)}, bf16[128,128]{1,0:T(8,128)(2,1)S(1)}, u32[]{:S(2)}, u32[]{:S(2)}) collective-permute-start(bf16[128,128]{1,0:T(8,128)(2,1)S(1)} %get-tuple-element.65), channel_id=1, source_target_pairs={{0,0},{1,2},{2,4},{3,6},{4,1},{5,3},{6,5},{7,7},{8,8},{9,10},{10,1... | collective-permute-start | bytes 98312 | tf_op jit(solution)/shard_map/ppermute | solution.py:111
  116.8 3.2 collective-permute-start.3
  120.1 3.2 collective-permute-done.3
  123.9 71.2 %all-gather.17.cloned.1.call-done.w_ref = bf16[32,27,16,256]{3,2,1,0:T(8,128)(2,1)} async-done(((bf16[8,27,16,256]{3,2,1,0:T(8,128)(2,1)}), bf16[32,27,16,256]{3,2,1,0:T(8,128)(2,1)}) %all-gather.17.cloned.1.call-update) | async-done | bytes 7077904 | tf_op jit(solution)/shard_map/all_gather | solution.py:133
  195.7 5.8 %conv_forward.8 = (bf16[256,128]{1,0:T(8,128)(2,1)}, f32[512,128]{1,0:T(8,128)}) custom-call(bf16[256,128]{1,0:T(8,128)(2,1)} %pad_maximum_fusion.2.x_ref, bf16[256,128]{1,0:T(8,128)(2,1)} %broadcast_in_dim.3.skip_ref, bf16[32,27,16,256]{3,2,1,0:T(8,128)(2,1)} %all-gather.17.cloned.1.call-done.w_ref), custom_call_target="tpu_custom_call" | custom-call | tf_op jit(solution)/shard_map/conv_forward/pallas_call | solution.py:154
  201.5 1.0 convert_element_type.179
  202.5 2.5 all-gather.2
  207.3 5.9 %conv_forward.9 = (bf16[256,128]{1,0:T(8,128)(2,1)}, f32[512,128]{1,0:T(8,128)}) custom-call(bf16[256,128]{1,0:T(8,128)(2,1)} %broadcast_select_fusion.6.x_ref, bf16[256,128]{1,0:T(8,128)(2,1)} %broadcast_in_dim.3.skip_ref, bf16[32,27,16,256]{3,2,1,0:T(8,128)(2,1)} %all-gather.17.cloned.1.call-done.w_ref), custom_call_target="tpu_custom_call" | custom-call | tf_op jit(solution)/shard_map/conv_forward/pallas_call | solution.py:154
  213.2 1.0 convert_element_type.184
  214.1 2.0 all-gather.3
  218.4 5.9 %conv_forward.10 = (bf16[256,128]{1,0:T(8,128)(2,1)}, f32[512,128]{1,0:T(8,128)}) custom-call(bf16[256,128]{1,0:T(8,128)(2,1)} %broadcast_select_fusion.5.x_ref, bf16[256,128]{1,0:T(8,128)(2,1)} %broadcast_in_dim.3.skip_ref, bf16[32,27,16,256]{3,2,1,0:T(8,128)(2,1)} %all-gather.17.cloned.1.call-done.w_ref), custom_call_target="tpu_custom_call" | custom-call | tf_op jit(solution)/shard_map/conv_forward/pallas_call | solution.py:154
  224.3 1.0 convert_element_type.189
  225.3 2.0 all-gather.4
  228.3 1.3 collective-permute-start.7
  229.6 11.6 %collective-permute-done.7 = bf16[256,128]{1,0:T(8,128)(2,1)S(1)} collective-permute-done((bf16[256,128]{1,0:T(8,128)(2,1)S(1)}, bf16[256,128]{1,0:T(8,128)(2,1)S(1)}, u32[]{:S(2)}, u32[]{:S(2)}) %collective-permute-start.7) | collective-permute-done | bytes 65568 | tf_op jit(solution)/shard_map/ppermute | solution.py:163
  241.8 5.9 %conv_forward.11 = (bf16[256,128]{1,0:T(8,128)(2,1)}, f32[512,128]{1,0:T(8,128)}) custom-call(bf16[256,128]{1,0:T(8,128)(2,1)} %broadcast_select_fusion.4.x_ref, bf16[256,128]{1,0:T(8,128)(2,1)} %broadcast_in_dim.3.skip_ref, bf16[32,27,16,256]{3,2,1,0:T(8,128)(2,1)} %all-gather.17.cloned.1.call-done.w_ref), custom_call_target="tpu_custom_call" | custom-call | tf_op jit(solution)/shard_map/conv_forward/pallas_call | solution.py:154
  247.7 1.0 convert_element_type.194
  248.7 2.6 all-gather.5
  252.2 1.3 collective-permute-start.8
  253.5 1.3 collective-permute-done.8.skip_ref
  255.5 5.9 %conv_forward.12 = (bf16[256,128]{1,0:T(8,128)(2,1)}, f32[512,128]{1,0:T(8,128)}) custom-call(bf16[256,128]{1,0:T(8,128)(2,1)} %broadcast_select_fusion.3.x_ref, bf16[256,128]{1,0:T(8,128)(2,1)} %copy-done, bf16[32,27,16,256]{3,2,1,0:T(8,128)(2,1)} %all-gather.17.cloned.1.call-done.w_ref), custom_call_target="tpu_custom_call" | custom-call | tf_op jit(solution)/shard_map/conv_forward/pallas_call | solution.py:154
  261.4 1.0 convert_element_type.199
  262.4 5.5 %all-gather.6 = bf16[1024,128]{1,0:T(8,128)(2,1)S(1)} all-gather(bf16[512,128]{1,0:T(8,128)(2,1)S(1)} %convert_element_type.199), channel_id=8, replica_groups=mesh['y'=4,'zh'=2,'zl'=8,'core'=2,'x'=4] {'core'}, dimensions={0}, use_global_device_ids=true | all-gather | bytes 393216 | tf_op jit(solution)/shard_map/all_gather | solution.py:119
  270.2 5.9 %conv_forward.13 = (bf16[256,128]{1,0:T(8,128)(2,1)}, f32[512,128]{1,0:T(8,128)}) custom-call(bf16[256,128]{1,0:T(8,128)(2,1)} %broadcast_select_fusion.2.x_ref, bf16[256,128]{1,0:T(8,128)(2,1)} %copy-done, bf16[32,27,16,256]{3,2,1,0:T(8,128)(2,1)} %all-gather.17.cloned.1.call-done.w_ref), custom_call_target="tpu_custom_call" | custom-call | tf_op jit(solution)/shard_map/conv_forward/pallas_call | solution.py:154
  276.0 1.0 convert_element_type.204
  277.0 2.0 all-gather.7
  280.7 9.1 %collective-permute-start = (bf16[128,128]{1,0:T(8,128)(2,1)S(1)}, bf16[128,128]{1,0:T(8,128)(2,1)S(1)}, u32[]{:S(2)}, u32[]{:S(2)}) collective-permute-start(bf16[128,128]{1,0:T(8,128)(2,1)S(1)} %get-tuple-element.71), channel_id=1, source_target_pairs={{0,56},{1,58},{2,60},{3,62},{4,57},{5,59},{6,61},{7,63},{8,48},{9,... | collective-permute-start | bytes 98312 | tf_op jit(solution)/shard_map/ppermute | solution.py:111
  289.8 3.4 collective-permute-start.1
  293.8 5.9 %conv_forward.14 = (bf16[256,128]{1,0:T(8,128)(2,1)}, f32[512,128]{1,0:T(8,128)}) custom-call(bf16[256,128]{1,0:T(8,128)(2,1)} %broadcast_select_fusion.1.x_ref, bf16[256,128]{1,0:T(8,128)(2,1)} %copy-done, bf16[32,27,16,256]{3,2,1,0:T(8,128)(2,1)} %all-gather.17.cloned.1.call-done.w_ref), custom_call_target="tpu_custom_call" | custom-call | tf_op jit(solution)/shard_map/conv_forward/pallas_call | solution.py:154
  299.7 1.0 convert_element_type.209
  300.7 2.5 all-gather.8
  305.5 5.8 %conv_forward.15 = (bf16[256,128]{1,0:T(8,128)(2,1)}, f32[512,128]{1,0:T(8,128)}) custom-call(bf16[256,128]{1,0:T(8,128)(2,1)} %broadcast_select_fusion.x_ref, bf16[256,128]{1,0:T(8,128)(2,1)} %copy-done, bf16[32,27,16,256]{3,2,1,0:T(8,128)(2,1)} %all-gather.17.cloned.1.call-done.w_ref), custom_call_target="tpu_custom_call" | custom-call | tf_op jit(solution)/shard_map/conv_forward/pallas_call | solution.py:154
  311.4 46.8 %all-gather.9 = bf16[2048,128]{1,0:T(8,128)(2,1)} all-gather(bf16[256,128]{1,0:T(8,128)(2,1)} %get-tuple-element.36), channel_id=11, replica_groups=mesh['y'=4,'zh'=2,'zl'=8,'core'=2,'x'=4] {'zl'}, dimensions={0}, use_global_device_ids=true | all-gather | bytes 589824 | tf_op jit(solution)/shard_map/all_gather | solution.py:166
  358.8 8.7 %all_gather.90.g_ref = bf16[512,128]{1,0:T(8,128)(2,1)} all-gather(bf16[256,128]{1,0:T(8,128)(2,1)S(1)} %get-tuple-element.68), channel_id=1, replica_groups=mesh['y'=4,'zh'=2,'zl'=8,'core'=2,'x'=4] {'core'}, dimensions={0}, use_global_device_ids=true | all-gather | bytes 196608 | tf_op jit(solution)/shard_map/all_gather | solution.py:173
  367.6 5.1 conv_backward.7
  374.0 2.0 all_gather.109.g_ref
  376.1 5.1 conv_backward.8
  382.6 2.0 all_gather.110.g_ref
  384.6 5.4 %conv_backward.9 = (bf16[256,128]{1,0:T(8,128)(2,1)}, bf16[256,128]{1,0:T(8,128)(2,1)}) custom-call(bf16[512,128]{1,0:T(8,128)(2,1)} %all_gather.110.g_ref, f32[256,128]{1,0:T(8,128)} %get-tuple-element.46.up_ref, bf16[256,128]{1,0:T(8,128)(2,1)} %broadcast_select_fusion.x_ref, bf16[256,128]{1,0:T(8,128)(2,1)} %copy-done, ...), custom_call_target="tpu_custom_call" | custom-call | tf_op jit(solution)/shard_map/conv_backward/pallas_call | solution.py:176
  391.4 2.0 all_gather.111.g_ref
  393.4 5.2 conv_backward.10
  399.5 1.3 collective-permute-start.15
  400.8 22.3 %collective-permute-done.15 = bf16[2,256,128]{2,1,0:T(8,128)(2,1)S(1)} collective-permute-done((bf16[2,256,128]{2,1,0:T(8,128)(2,1)S(1)}, bf16[2,256,128]{2,1,0:T(8,128)(2,1)S(1)}, u32[]{:S(2)}, u32[]{:S(2)}) %collective-permute-start.15) | collective-permute-done | bytes 131104 | tf_op jit(solution)/shard_map/ppermute | solution.py:178
  423.8 2.7 all_gather.112.g_ref
  426.5 5.1 conv_backward.11
  431.6 1.3 collective-permute-start.16
  432.9 1.6 collective-permute-done.16
  435.2 2.9 all_gather.113.g_ref
  438.1 5.1 conv_backward.12
  444.6 2.2 all_gather.114.g_ref
  446.8 5.1 conv_backward.13
  452.7 1.9 all_gather.115
  454.6 7.2 %all_to_all.31 = bf16[4,8,16,128]{3,2,1,0:T(8,128)(2,1)S(1)} all-to-all(bf16[4,8,16,128]{3,2,1,0:T(8,128)(2,1)S(1)} %bitcast.53), channel_id=1, replica_groups=mesh['y'=4,'zh'=2,'zl'=8,'core'=2,'x'=4] {'x'}, dimensions={0} | all-to-all | bytes 262144 | tf_op jit(solution)/shard_map/all_to_all | solution.py:189
  461.8 16.9 %all_to_all.32 = bf16[4,8,16,128]{3,2,0,1:T(8,128)(2,1)S(1)} all-to-all(bf16[4,8,16,128]{3,2,0,1:T(8,128)(2,1)S(1)} %copy.15), channel_id=1, replica_groups=mesh['y'=4,'zh'=2,'zl'=8,'core'=2,'x'=4] {'zl'}, dimensions={1} | all-to-all | bytes 262144 | tf_op jit(solution)/shard_map/all_to_all | solution.py:190
  479.4 3.8 weight_grad.1
  484.1 7.2 %all_to_all.33 = bf16[27,2,8,256]{3,2,0,1:T(8,128)(2,1)S(1)} all-to-all(bf16[27,2,8,256]{3,2,0,1:T(8,128)(2,1)S(1)} %copy.17), channel_id=1, replica_groups=mesh['y'=4,'zh'=2,'zl'=8,'core'=2,'x'=4] {'core'}, dimensions={1} | all-to-all | bytes 442368 | tf_op jit(solution)/shard_map/all_to_all | solution.py:196
  491.3 1.9 collective-permute-start.19
  493.3 32.1 %collective-permute-done.19 = bf16[27,2,8,256]{3,2,0,1:T(8,128)(2,1)S(1)} collective-permute-done((bf16[27,2,8,256]{3,2,0,1:T(8,128)(2,1)S(1)}, bf16[27,2,8,256]{3,2,0,1:T(8,128)(2,1)S(1)}, u32[]{:S(2)}, u32[]{:S(2)}) %collective-permute-start.19) | collective-permute-done | bytes 221216 | tf_op jit(solution)/shard_map/ppermute | solution.py:199
  525.7 1.1 reshape.92
  (105 shorter events, 27.7 us)
Async XLA Ops:
  6.5 102.3 %copy-start.14 = (bf16[2,128,128]{2,1,0:T(8,128)(2,1)S(1)}, bf16[2,128,128]{2,1,0:T(8,128)(2,1)}, u32[]{:S(2)}) copy-start(bf16[2,128,128]{2,1,0:T(8,128)(2,1)} %param.3) | copy-start | bytes 196612
  6.5 102.2 %all-gather.15.cloned.1.call-start = ((), (), s32[]{:S(2)}) async-start(), calls=%async_computation.4 | async-start | bytes 1990656 | tf_op jit(solution)/shard_map/all_gather | solution.py:132
  11.8 34.9 %collective-permute-start.4 = (bf16[27,16,256]{2,1,0:T(8,128)(2,1)S(1)}, bf16[27,16,256]{2,1,0:T(8,128)(2,1)S(1)}, u32[]{:S(2)}, u32[]{:S(2)}) collective-permute-start(bf16[27,16,256]{2,1,0:T(8,128)(2,1)S(1)} %bitcast.55), channel_id=1, source_target_pairs={{0,0},{64,128},{128,256},{192,384},{256,448},{320,320},{384,192},{... | collective-permute-start | bytes 663560 | tf_op jit(solution)/shard_map/ppermute | solution.py:131
  46.7 0.7 copy-start.13
  47.4 147.6 %all-gather.17.cloned.1.call-start = ((), (), s32[]{:S(2)}) async-start(), calls=%async_computation.5 | async-start | bytes 8847360 | tf_op jit(solution)/shard_map/all_gather | solution.py:133
  108.8 370.6 %all-gather.19.cloned.1.call-start = ((), (), s32[]{:S(2)}) async-start(), calls=%async_computation.6 | async-start | bytes 2621440 | tf_op jit(solution)/shard_map/all_gather | solution.py:167
  108.9 11.2 %collective-permute-start.2 = (bf16[128,128]{1,0:T(8,128)(2,1)S(1)}, bf16[128,128]{1,0:T(8,128)(2,1)S(1)}, u32[]{:S(2)}, u32[]{:S(2)}) collective-permute-start(bf16[128,128]{1,0:T(8,128)(2,1)S(1)} %get-tuple-element.65), channel_id=1, source_target_pairs={{0,0},{1,2},{2,4},{3,6},{4,1},{5,3},{6,5},{7,7},{8,8},{9,10},{10,1... | collective-permute-start | bytes 98312 | tf_op jit(solution)/shard_map/ppermute | solution.py:111
  116.8 6.4 %collective-permute-start.3 = (bf16[128,128]{1,0:T(8,128)(2,1)S(1)}, bf16[128,128]{1,0:T(8,128)(2,1)S(1)}, u32[]{:S(2)}, u32[]{:S(2)}) collective-permute-start(bf16[128,128]{1,0:T(8,128)(2,1)S(1)} %get-tuple-element.66), channel_id=1, source_target_pairs={{0,2},{1,0},{2,6},{3,4},{4,3},{5,1},{6,7},{7,5},{8,10},{9,8},{10,1... | collective-permute-start | bytes 98312 | tf_op jit(solution)/shard_map/ppermute | solution.py:111
  205.9 0.7 collective-permute-start.5
  207.3 8.9 %copy-start.9 = (bf16[256,128]{1,0:T(8,128)(2,1)S(1)}, bf16[256,128]{1,0:T(8,128)(2,1)}, u32[]{:S(2)}) copy-start(bf16[256,128]{1,0:T(8,128)(2,1)} %broadcast_select_fusion.6.x_ref) | copy-start | bytes 196612
  217.1 0.7 collective-permute-start.6
  218.4 8.9 %copy-start.10 = (bf16[256,128]{1,0:T(8,128)(2,1)S(1)}, bf16[256,128]{1,0:T(8,128)(2,1)}, u32[]{:S(2)}) copy-start(bf16[256,128]{1,0:T(8,128)(2,1)} %broadcast_select_fusion.5.x_ref) | copy-start | bytes 196612
  228.3 12.9 %collective-permute-start.7 = (bf16[256,128]{1,0:T(8,128)(2,1)S(1)}, bf16[256,128]{1,0:T(8,128)(2,1)S(1)}, u32[]{:S(2)}, u32[]{:S(2)}) collective-permute-start(bf16[256,128]{1,0:T(8,128)(2,1)S(1)} %fusion.14), channel_id=1, source_target_pairs={{256,384},{257,385},{258,386},{259,387},{260,388},{261,389},{262,3... | collective-permute-start | bytes 196616 | tf_op jit(solution)/shard_map/ppermute | solution.py:163
  241.8 9.4 %copy-start.11 = (bf16[256,128]{1,0:T(8,128)(2,1)S(1)}, bf16[256,128]{1,0:T(8,128)(2,1)}, u32[]{:S(2)}) copy-start(bf16[256,128]{1,0:T(8,128)(2,1)} %broadcast_select_fusion.4.x_ref) | copy-start | bytes 196612
  252.2 2.6 collective-permute-start.8
  254.8 0.7 copy-start
  255.5 12.4 %copy-start.12 = (bf16[256,128]{1,0:T(8,128)(2,1)S(1)}, bf16[256,128]{1,0:T(8,128)(2,1)}, u32[]{:S(2)}) copy-start(bf16[256,128]{1,0:T(8,128)(2,1)} %broadcast_select_fusion.3.x_ref) | copy-start | bytes 196612
  268.8 0.7 collective-permute-start.9
  270.2 8.9 %copy-start.7 = (bf16[256,128]{1,0:T(8,128)(2,1)S(1)}, bf16[256,128]{1,0:T(8,128)(2,1)}, u32[]{:S(2)}) copy-start(bf16[256,128]{1,0:T(8,128)(2,1)} %broadcast_select_fusion.2.x_ref) | copy-start | bytes 196612
  270.2 10.5 %copy-start.15 = (bf16[2,128,128]{2,1,0:T(8,128)(2,1)S(1)}, bf16[2,128,128]{2,1,0:T(8,128)(2,1)}, u32[]{:S(2)}) copy-start(bf16[2,128,128]{2,1,0:T(8,128)(2,1)} %param.5) | copy-start | bytes 196612
  280.0 13.2 %collective-permute-start.10 = (bf16[256,128]{1,0:T(8,128)(2,1)S(1)}, bf16[256,128]{1,0:T(8,128)(2,1)S(1)}, u32[]{:S(2)}, u32[]{:S(2)}) collective-permute-start(bf16[256,128]{1,0:T(8,128)(2,1)S(1)} %fusion.8), channel_id=1, source_target_pairs={{320,192},{321,193},{322,194},{323,195},{324,196},{325,197},{326,1... | collective-permute-start | bytes 196616 | tf_op jit(solution)/shard_map/ppermute | solution.py:163
  280.7 24.1 %collective-permute-start = (bf16[128,128]{1,0:T(8,128)(2,1)S(1)}, bf16[128,128]{1,0:T(8,128)(2,1)S(1)}, u32[]{:S(2)}, u32[]{:S(2)}) collective-permute-start(bf16[128,128]{1,0:T(8,128)(2,1)S(1)} %get-tuple-element.71), channel_id=1, source_target_pairs={{0,56},{1,58},{2,60},{3,62},{4,57},{5,59},{6,61},{7,63},{8,48},{9,... | collective-permute-start | bytes 98312 | tf_op jit(solution)/shard_map/ppermute | solution.py:111
  289.8 15.0 %collective-permute-start.1 = (bf16[128,128]{1,0:T(8,128)(2,1)S(1)}, bf16[128,128]{1,0:T(8,128)(2,1)S(1)}, u32[]{:S(2)}, u32[]{:S(2)}) collective-permute-start(bf16[128,128]{1,0:T(8,128)(2,1)S(1)} %get-tuple-element.72), channel_id=1, source_target_pairs={{0,58},{1,56},{2,62},{3,60},{4,59},{5,57},{6,63},{7,61},{8,50},{9,... | collective-permute-start | bytes 98312 | tf_op jit(solution)/shard_map/ppermute | solution.py:111
  293.8 9.4 %copy-start.8 = (bf16[256,128]{1,0:T(8,128)(2,1)S(1)}, bf16[256,128]{1,0:T(8,128)(2,1)}, u32[]{:S(2)}) copy-start(bf16[256,128]{1,0:T(8,128)(2,1)} %broadcast_select_fusion.1.x_ref) | copy-start | bytes 196612
  304.2 0.7 collective-permute-start.11
  372.7 0.7 collective-permute-start.12
  376.1 5.8 %copy-start.2 = (f32[256,128]{1,0:T(8,128)S(1)}, f32[256,128]{1,0:T(8,128)}, u32[]{:S(2)}) copy-start(f32[256,128]{1,0:T(8,128)} %get-tuple-element.48.up_ref) | copy-start | bytes 393220
  381.2 0.7 collective-permute-start.13
  384.6 6.1 %copy-start.4 = (f32[256,128]{1,0:T(8,128)S(1)}, f32[256,128]{1,0:T(8,128)}, u32[]{:S(2)}) copy-start(f32[256,128]{1,0:T(8,128)} %get-tuple-element.46.up_ref) | copy-start | bytes 393220
  390.0 0.7 collective-permute-start.14
  393.4 29.7 %copy-start.1 = (f32[256,128]{1,0:T(8,128)S(1)}, f32[256,128]{1,0:T(8,128)}, u32[]{:S(2)}) copy-start(f32[256,128]{1,0:T(8,128)} %get-tuple-element.44.up_ref) | copy-start | bytes 393220
  399.5 23.6 %collective-permute-start.15 = (bf16[2,256,128]{2,1,0:T(8,128)(2,1)S(1)}, bf16[2,256,128]{2,1,0:T(8,128)(2,1)S(1)}, u32[]{:S(2)}, u32[]{:S(2)}) collective-permute-start(bf16[2,256,128]{2,1,0:T(8,128)(2,1)S(1)} %pad_maximum_fusion), channel_id=1, source_target_pairs={{120,0},{112,8},{104,16},{96,24},{88,32},{80,40},{72,48},{64,56},{... | collective-permute-start | bytes 393224 | tf_op jit(solution)/shard_map/ppermute | solution.py:178
  426.5 8.1 %copy-start.5 = (f32[256,128]{1,0:T(8,128)S(1)}, f32[256,128]{1,0:T(8,128)}, u32[]{:S(2)}) copy-start(f32[256,128]{1,0:T(8,128)} %get-tuple-element.42.up_ref) | copy-start | bytes 393220
  431.6 2.9 collective-permute-start.16
  438.1 5.8 %copy-start.6 = (f32[256,128]{1,0:T(8,128)S(1)}, f32[256,128]{1,0:T(8,128)}, u32[]{:S(2)}) copy-start(f32[256,128]{1,0:T(8,128)} %get-tuple-element.40.up_ref) | copy-start | bytes 393220
  443.2 0.7 collective-permute-start.17
  446.8 5.8 %copy-start.3 = (f32[256,128]{1,0:T(8,128)S(1)}, f32[256,128]{1,0:T(8,128)}, u32[]{:S(2)}) copy-start(f32[256,128]{1,0:T(8,128)} %get-tuple-element.38.up_ref) | copy-start | bytes 393220
  451.9 0.7 collective-permute-start.18
  491.3 34.1 %collective-permute-start.19 = (bf16[27,2,8,256]{3,2,0,1:T(8,128)(2,1)S(1)}, bf16[27,2,8,256]{3,2,0,1:T(8,128)(2,1)S(1)}, u32[]{:S(2)}, u32[]{:S(2)}) collective-permute-start(bf16[27,2,8,256]{3,2,0,1:T(8,128)(2,1)S(1)} %all_to_all.33), channel_id=1, source_target_pairs={{0,0},{128,64},{256,128},{384,192},{448,256},{320,320},{192,384},{... | collective-permute-start | bytes 663560 | tf_op jit(solution)/shard_map/ppermute | solution.py:199
Sparse Core Ops, SparseCore 0:
  47.5 61.1 all-gather.14
  110.9 84.1 all-gather.16
  358.3 49.7 all-gather.18

commit v2 on v1

--- a/solution.py
+++ b/solution.py
@@ -24,27 +24,46 @@
     return jnp.where(inside, turned, 0.0)
 
 
-def forward_kernel(x_ref, skip_ref, w_ref, act_ref, out_ref):
+def conv(matrix_of, stacks):
+    total = None
+    for j, stacked in enumerate(stacks):
+        part = lax.dot_general(
+            matrix_of(3 * j), stacked, (((1,), (0,)), ((), ())), preferred_element_type=F32
+        )
+        total = part if total is None else total + part
+    return total
+
+
+def forward_kernel(core_ref, x_ref, skip_ref, w_ref, act_ref, own_ref, other_ref):
+    core = core_ref[0]
     summed = x_ref[...].astype(F32) + skip_ref[...].astype(F32)
     act = (summed * jax.nn.sigmoid(summed)).astype(BF16)
     act_ref[...] = act
     act = act.astype(F32)
-    total = None
-    for first in range(0, 27, 3):
-        stacked = jnp.concatenate(
+    stacks = [
+        jnp.concatenate(
             [shifted(act, TAPS[k]).astype(BF16) for k in range(first, first + 3)], axis=0
         )
-        matrix = jnp.concatenate(
-            [w_ref[:, k].reshape(512, 256) for k in range(first, first + 3)], axis=1
-        )
-        part = lax.dot_general(
-            matrix, stacked, (((1,), (0,)), ((), ())), preferred_element_type=F32
-        )
-        total = part if total is None else total + part
-    out_ref[...] = total
-
-
-def backward_kernel(g_ref, up_ref, x_ref, skip_ref, w_ref, sent_ref, pre_ref, pad_ref):
+        for first in range(0, 27, 3)
+    ]
+
+    def rows(half):
+        def matrix_of(first):
+            return jnp.concatenate(
+                [
+                    w_ref[pl.ds(half * 16, 16), k].reshape(256, 256)
+                    for k in range(first, first + 3)
+                ],
+                axis=1,
+            )
+
+        return conv(matrix_of, stacks)
+
+    other_ref[...] = rows(1 - core).astype(BF16)
+    own_ref[...] = rows(core)
+
+
+def backward_kernel(g_ref, up_ref, gskip_ref, x_ref, skip_ref, w_ref, sent_ref, pre_ref, pad_ref):
     grads = g_ref[...].astype(F32).T
     column = lax.broadcasted_iota(jnp.int32, (CELLS, 1), 0) % 8
     pad_ref[...] = jnp.zeros(pad_ref.shape, F32)
@@ -68,26 +87,32 @@
     sig = jax.nn.sigmoid(summed)
     pre = total.T * (sig * (1.0 + summed * (1.0 - sig)))
     pre_ref[...] = pre.astype(BF16)
-    sent_ref[...] = (up_ref[...] + pre).astype(BF16)
-
-
-def weight_grad_kernel(g_ref, a_ref, out_ref):
+    upstream = up_ref[...].astype(F32) + gskip_ref[...].astype(F32)
+    sent_ref[...] = (upstream + pre).astype(BF16)
+
+
+def weight_grad_kernel(x_ref, g_ref, a_ref, out_ref):
+    x = x_ref[0]
     total = None
-    for v in range(0, 32, 2):
-        rows = []
-        for u in (v, v + 1):
-            grads = g_ref[u].astype(F32)
-            rows.append(
-                jnp.concatenate(
-                    [shifted(grads, tuple(-m for m in move)).astype(BF16) for move in TAPS], axis=0
+    for z in range(8):
+        for pair in range(2):
+            left, right = [], []
+            for column in (2 * pair, 2 * pair + 1):
+                grads = g_ref[column * 8 + z].astype(F32)
+                left.append(
+                    jnp.concatenate(
+                        [shifted(grads, tuple(-m for m in move)).astype(BF16) for move in TAPS],
+                        axis=0,
+                    )
                 )
+                right.append(a_ref[z, (x - column + 4) % 4])
+            part = lax.dot_general(
+                jnp.concatenate(left, axis=1),
+                jnp.concatenate(right, axis=1),
+                (((1,), (1,)), ((), ())),
+                preferred_element_type=F32,
             )
-        left = jnp.concatenate(rows, axis=1)
-        right = jnp.concatenate([a_ref[v], a_ref[v + 1]], axis=1)
-        part = lax.dot_general(
-            left, right, (((1,), (1,)), ((), ())), preferred_element_type=F32
-        )
-        total = part if total is None else total + part
+            total = part if total is None else total + part
     out_ref[...] = total.astype(BF16)
 
 
@@ -115,9 +140,8 @@
     )
 
 
-def other_partial(partial, core):
-    both = lax.all_gather(partial.astype(BF16), "core", axis=0, tiled=False)
-    return own_half(jnp.where(core == 0, both[1], both[0]), core)
+def near(*arrays):
+    return [pltpu.with_memory_space_constraint(array, pltpu.VMEM) for array in arrays]
 
 
 def on_device(clips, weights, cotangents):
@@ -135,26 +159,35 @@
     x_hold = volume_half(clips, core, x, False)
     carried = volume_half(cotangents, core, x, True)
 
-    tile = jax.ShapeDtypeStruct((256, CELLS), BF16)
+    kernel = near(kernel)[0]
+    tile = pltpu.VMEM((256, CELLS), BF16)
+    limits = pltpu.CompilerParams(vmem_limit_bytes=20 * 1024 * 1024)
+    everywhere = pl.BlockSpec(memory_space=pltpu.VMEM)
+    scalar = pl.BlockSpec(memory_space=pltpu.SMEM)
     forward = pl.pallas_call(
         forward_kernel,
-        out_shape=(tile, jax.ShapeDtypeStruct((512, CELLS), F32)),
+        in_specs=[scalar] + [everywhere] * 3,
+        out_shape=(tile, pltpu.VMEM((256, CELLS), F32), tile),
+        compiler_params=limits,
         name="conv_forward",
     )
     backward = pl.pallas_call(
         backward_kernel,
         out_shape=(tile, tile),
         scratch_shapes=(pltpu.VMEM((3, 6, 6, 8, 512), F32),),
+        compiler_params=limits,
         name="conv_backward",
     )
+    core_at = core.astype(jnp.int32).reshape(1)
     across = [(z, 15 - z) for z in range(8)]
 
     skip = jnp.zeros((256, CELLS), BF16)
     for l in range(LAYERS):
-        act, partial = forward(x_hold, skip, kernel)
+        act, mine, other = forward(core_at, *near(x_hold, skip, kernel))
         if l == LAYERS - 1:
             break
-        update = own_half(partial, core) + other_partial(partial, core).astype(F32)
+        both = lax.all_gather(other, "core", axis=0, tiled=False)
+        update = mine + jnp.where(core == 0, both[1], both[0]).astype(F32)
         out = (x_hold.astype(F32) + update).astype(BF16)
         if l == 3:
             skip = lax.ppermute(out, ("zh", "zl"), across)
@@ -163,36 +196,38 @@
             got = lax.ppermute(out, section, [(PLACE[l], PLACE[l + 1])])
             x_hold = jnp.where(layer == l + 1, got, x_hold)
 
-    acts = lax.all_gather(act, "zl", axis=0, tiled=False)
-    acts = lax.all_gather(acts, "x", axis=0, tiled=False).reshape(32, 256, CELLS)
+    acts = jnp.stack(
+        [act] + [lax.ppermute(act, "x", [(i, (i + turn) % 4) for i in range(4)]) for turn in (1, 2, 3)]
+    )
+    acts = lax.all_gather(acts, "zl", axis=0, tiled=False)
 
     back = [(b, a) for a, b in across]
-    upstream = carried.astype(F32)
+    gskip = jnp.zeros((256, CELLS), BF16)
     for l in reversed(range(LAYERS)):
-        low = upstream.astype(BF16)
+        low = (carried.astype(F32) + gskip.astype(F32)).astype(BF16)
         grads = lax.all_gather(low, "core", axis=0, tiled=True)
         if l == 0:
             break
-        sent, pre = backward(grads, upstream, x_hold, skip, kernel)
+        sent, pre = backward(*near(grads, carried, gskip, x_hold, skip, kernel))
         if l == 4:
-            both = lax.ppermute(jnp.stack([sent, pre]), ("zh", "zl"), back)
-            gskip = both[1].astype(F32)
-            upstream = jnp.where(layer < 4, gskip, upstream)
-            upstream = jnp.where(layer == 3, both[0].astype(F32) + gskip, upstream)
+            whole = (sent.astype(F32) + pre.astype(F32)).astype(BF16)
+            got = lax.ppermute(jnp.where(layer == 4, whole, pre), ("zh", "zl"), back)
+            carried = jnp.where(layer == 3, got, carried)
+            gskip = jnp.where(layer < 3, got, gskip)
         else:
-            got = lax.ppermute(sent, section, [(PLACE[l], PLACE[l - 1])]).astype(F32)
-            if l < 4:
-                got = got + gskip
-            upstream = jnp.where(layer == l - 1, got, upstream)
+            got = lax.ppermute(sent, section, [(PLACE[l], PLACE[l - 1])])
+            carried = jnp.where(layer == l - 1, got, carried)
 
     rows = grads.reshape(4, 8, 16, CELLS)
     rows = lax.all_to_all(rows, "x", split_axis=0, concat_axis=0)
     rows = lax.all_to_all(rows, "zl", split_axis=1, concat_axis=1).reshape(32, 16, CELLS)
     total = pl.pallas_call(
         weight_grad_kernel,
-        out_shape=jax.ShapeDtypeStruct((432, 256), BF16),
+        in_specs=[scalar] + [everywhere] * 2,
+        out_shape=pltpu.VMEM((432, 256), BF16),
+        compiler_params=limits,
         name="weight_grad",
-    )(rows, acts)
+    )(x.astype(jnp.int32).reshape(1), rows, acts)
     total = lax.all_to_all(
         total.reshape(27, 2, 8, 256), "core", split_axis=1, concat_axis=1
     )

time: 535 us -> 467 us (0.87)
  blocking collectives: 126 us -> 66.4 us
  Pallas kernels: 87.1 us -> 35.1 us
  waiting for transfers between devices: 224 us -> 254 us
  local copies, waits for them, and re-layouts: 5.52 us -> 34.8 us
  other arithmetic: 24.3 us -> 1.38 us
  starting transfers between devices: 52.6 us -> 60.6 us
    pallas_call x16, Pallas kernels: 87.1 us -> 35.1 us  [the longest x8 21.4 us: on_device(): act, mine, other = forward(core_at, *near(x_hold, skip, kernel))]
    all_gather x8 -> x7, blocking collectives: 65.8 us -> 17.8 us  [on_device(): both = lax.all_gather(other, 'core', axis=0, tiled=False)]
    unnamed x32 -> x28, local copies, waits for them, and re-layouts: 0.74 us -> 32.3 us
    ppermute x7 -> x10, waiting for transfers between devices: 23.9 us -> 43.6 us  [the longest x1 38.3 us: on_device(): got = lax.ppermute(jnp.where(layer == 4, whole, pre), ('zh', 'zl'), back)]
    convert_element_type x15 -> x4, other arithmetic: 11.5 us -> 0.14 us  [on_device(): low = (carried.astype(F32) + gskip.astype(F32)).astype(BF16)]
    ppermute x4, waiting for transfers between devices: 3.2 us -> 12.6 us  [volume_half(): got.append(lax.ppermute(picked[turn], ('zl', 'core', 'x'), route))]
    ppermute x7 -> x10, starting transfers between devices: 5.84 us -> 14.6 us  [the longest x3 8.79 us: on_device(): lax.ppermute(act, 'x', [(i, (i + turn) % 4) for i in range(4)])]
    all_gather x8, blocking collectives: 24.5 us -> 16.7 us  [on_device(): grads = lax.all_gather(low, 'core', axis=0, tiled=True)]
  transfers between devices with their start and end apart: 23 -> 26, of which waited for: 9 -> 13; matrix products, arithmetic and copies ran while one was open for 2% -> 0% of each run, Pallas kernels for 8% -> 3%
where the time goes in v2:
time: 467 us; the launch traced here: 466 us
  waiting for transfers between devices  254 us (54%)
  blocking collectives  66.4 us (14%)
  starting transfers between devices  60.6 us (13%)
  Pallas kernels  35.1 us (8%)
  local copies, waits for them, and re-layouts  34.8 us (7%)
  between operations  13.8 us (3%)
    all_gather x1, waiting for transfers between devices, on_device(): lax.all_gather(kernel, 'x', axis=0, tiled=False).reshape(32, 27, 16, 256)  71.8 us
    all_gather x1, waiting for transfers between devices, on_device(): kernel = lax.all_gather(own, 'zl', axis=0, tiled=False)  61.3 us
    ppermute x1, waiting for transfers between devices, on_device(): got = lax.ppermute(jnp.where(layer == 4, whole, pre), ('zh', 'zl'), back)  38.3 us
    unnamed x28, local copies, waits for them, and re-layouts  32.3 us
    ppermute x1, waiting for transfers between devices, on_device(): total = lax.ppermute(total, section, [(PLACE[l], l) for l in range(LAYERS)])  32.1 us
    ppermute x4, starting transfers between devices, volume_half(): got.append(lax.ppermute(picked[turn], ('zl', 'core', 'x'), route))  22.7 us
    pallas_call x8, Pallas kernels, on_device(): act, mine, other = forward(core_at, *near(x_hold, skip, kernel))  21.4 us
    ppermute x1, waiting for transfers between devices, on_device(): own = lax.ppermute(own, section, [(l, PLACE[l]) for l in range(LAYERS)])  19.6 us
  transfers between devices with their start and end apart: 26, of which 13 were waited for; matrix products, arithmetic and copies ran while one was open for 0% of the time, Pallas kernels for 3%

profile of v2, /device:TPU:57, one launch (start us, length us, event | category | flops | bytes accessed | tf_op | source)
XLA Modules:
  0.0 466.1 jit_solution(17141627320985881177)
XLA Ops:
  7.6 4.2 all_to_all.30
  11.8 15.2 %collective-permute-start.4 = (bf16[27,16,256]{2,1,0:T(8,128)(2,1)S(1)}, bf16[27,16,256]{2,1,0:T(8,128)(2,1)S(1)}, u32[]{:S(2)}, u32[]{:S(2)}) collective-permute-start(bf16[27,16,256]{2,1,0:T(8,128)(2,1)S(1)} %bitcast.40), channel_id=1, source_target_pairs={{0,0},{64,128},{128,256},{192,384},{256,448},{320,320},{384,192},{... | collective-permute-start | bytes 663560 | tf_op jit(solution)/shard_map/ppermute | solution.py:155
  27.0 19.6 %collective-permute-done.4 = bf16[27,16,256]{2,1,0:T(8,128)(2,1)S(1)} collective-permute-done((bf16[27,16,256]{2,1,0:T(8,128)(2,1)S(1)}, bf16[27,16,256]{2,1,0:T(8,128)(2,1)S(1)}, u32[]{:S(2)}, u32[]{:S(2)}) %collective-permute-start.4) | collective-permute-done | bytes 221216 | tf_op jit(solution)/shard_map/ppermute | solution.py:155
  47.5 61.3 %all-gather.14.cloned.1.call-done = bf16[216,16,256]{2,1,0:T(8,128)(2,1)} async-done(((bf16[27,16,256]{2,1,0:T(8,128)(2,1)}), bf16[216,16,256]{2,1,0:T(8,128)(2,1)}) %all-gather.14.cloned.1.call-update) | async-done | bytes 1769488 | tf_op jit(solution)/shard_map/all_gather | solution.py:156
  108.9 7.9 %collective-permute-start.2 = (bf16[128,128]{1,0:T(8,128)(2,1)S(1)}, bf16[128,128]{1,0:T(8,128)(2,1)S(1)}, u32[]{:S(2)}, u32[]{:S(2)}) collective-permute-start(bf16[128,128]{1,0:T(8,128)(2,1)S(1)} %get-tuple-element.60), channel_id=1, source_target_pairs={{0,0},{1,2},{2,4},{3,6},{4,1},{5,3},{6,5},{7,7},{8,8},{9,10},{10,1... | collective-permute-start | bytes 98312 | tf_op jit(solution)/shard_map/ppermute | solution.py:136
  116.8 3.2 collective-permute-start.3
  120.1 3.2 collective-permute-done.3
  123.3 71.8 %all-gather.16.cloned.1.call-done.w_ref = bf16[32,27,16,256]{3,2,1,0:T(8,128)(2,1)} async-done(((bf16[8,27,16,256]{3,2,1,0:T(8,128)(2,1)}), bf16[32,27,16,256]{3,2,1,0:T(8,128)(2,1)}) %all-gather.16.cloned.1.call-update) | async-done | bytes 7077904 | tf_op jit(solution)/shard_map/all_gather | solution.py:157
  195.1 3.0 copy-done
  198.1 2.7 conv_forward.8
  200.7 2.4 all-gather.2
  203.9 3.0 copy-done.1
  206.9 2.6 conv_forward.9
  209.5 1.9 all-gather.3
  212.2 3.0 copy-done.2
  215.2 2.7 conv_forward.10
  217.8 1.9 all-gather.4
  221.1 11.6 %collective-permute-done.7 = bf16[256,128]{1,0:T(8,128)(2,1)S(1)} collective-permute-done((bf16[256,128]{1,0:T(8,128)(2,1)S(1)}, bf16[256,128]{1,0:T(8,128)(2,1)S(1)}, u32[]{:S(2)}, u32[]{:S(2)}) %collective-permute-start.7) | collective-permute-done | bytes 65568 | tf_op jit(solution)/shard_map/ppermute | solution.py:196
  232.7 3.0 copy-done.3
  235.7 2.7 conv_forward.11
  238.4 2.5 all-gather.5
  240.9 1.5 collective-permute-start.8
  243.5 3.0 copy-done.4
  246.5 2.7 conv_forward.12
  249.2 5.4 %all-gather.6 = bf16[512,128]{1,0:T(8,128)(2,1)S(1)} all-gather(bf16[256,128]{1,0:T(8,128)(2,1)S(1)} %get-tuple-element.37), channel_id=8, replica_groups=mesh['y'=4,'zh'=2,'zl'=8,'core'=2,'x'=4] {'core'}, dimensions={0}, use_global_device_ids=true | all-gather | bytes 196608 | tf_op jit(solution)/shard_map/all_gather | solution.py:189
  255.3 3.0 copy-done.5
  258.3 2.7 conv_forward.13
  261.0 1.9 all-gather.7
  263.6 3.0 copy-done.6
  266.6 2.7 conv_forward.14
  269.3 1.9 all-gather.8
  271.9 3.0 copy-done.7
  274.9 2.8 conv_forward.15
  277.7 3.2 collective-permute-start.21
  280.9 3.4 collective-permute-start.20
  284.3 2.2 collective-permute-start.19
  287.4 3.1 collective-permute-done.19
  291.3 8.9 %collective-permute-start = (bf16[128,128]{1,0:T(8,128)(2,1)S(1)}, bf16[128,128]{1,0:T(8,128)(2,1)S(1)}, u32[]{:S(2)}, u32[]{:S(2)}) collective-permute-start(bf16[128,128]{1,0:T(8,128)(2,1)S(1)} %get-tuple-element.64), channel_id=1, source_target_pairs={{0,56},{1,58},{2,60},{3,62},{4,57},{5,59},{6,61},{7,63},{8,48},{9,... | collective-permute-start | bytes 98312 | tf_op jit(solution)/shard_map/ppermute | solution.py:136
  300.2 2.7 collective-permute-start.1
  303.8 8.6 %collective-permute-done.1 = bf16[128,128]{1,0:T(8,128)(2,1)S(1)} collective-permute-done((bf16[128,128]{1,0:T(8,128)(2,1)S(1)}, bf16[128,128]{1,0:T(8,128)(2,1)S(1)}, u32[]{:S(2)}, u32[]{:S(2)}) %collective-permute-start.1) | collective-permute-done | bytes 32800 | tf_op jit(solution)/shard_map/ppermute | solution.py:136
  312.4 2.5 all_gather.84.g_ref
  314.9 3.0 copy-done.8
  317.9 1.8 conv_backward.7
  320.5 2.1 all_gather.103.g_ref
  322.6 1.9 conv_backward.8
  325.1 1.9 all_gather.104.g_ref
  327.0 1.8 conv_backward.9
  329.6 1.9 all_gather.105.g_ref
  334.1 38.3 %collective-permute-done.15 = bf16[256,128]{1,0:T(8,128)(2,1)S(1)} collective-permute-done((bf16[256,128]{1,0:T(8,128)(2,1)S(1)}, bf16[256,128]{1,0:T(8,128)(2,1)S(1)}, u32[]{:S(2)}, u32[]{:S(2)}) %collective-permute-start.15) | collective-permute-done | bytes 65568 | tf_op jit(solution)/shard_map/ppermute | solution.py:214
  372.4 1.9 all_gather.106.g_ref
  374.3 3.0 copy-done.9
  377.3 1.8 conv_backward.11
  381.8 2.5 all_gather.107.g_ref
  384.3 1.8 conv_backward.12
  386.9 1.9 all_gather.108.g_ref
  388.8 1.8 conv_backward.13
  391.3 1.9 all_gather.109
  393.2 7.2 %all_to_all.31 = bf16[4,8,16,128]{3,2,1,0:T(8,128)(2,1)S(1)} all-to-all(bf16[4,8,16,128]{3,2,1,0:T(8,128)(2,1)S(1)} %bitcast.38), channel_id=1, replica_groups=mesh['y'=4,'zh'=2,'zl'=8,'core'=2,'x'=4] {'x'}, dimensions={0} | all-to-all | bytes 262144 | tf_op jit(solution)/shard_map/all_to_all | solution.py:222
  400.5 13.1 %all_to_all.32 = bf16[4,8,16,128]{3,2,0,1:T(8,128)(2,1)S(1)} all-to-all(bf16[4,8,16,128]{3,2,0,1:T(8,128)(2,1)S(1)} %copy.15), channel_id=1, replica_groups=mesh['y'=4,'zh'=2,'zl'=8,'core'=2,'x'=4] {'zl'}, dimensions={1} | all-to-all | bytes 262144 | tf_op jit(solution)/shard_map/all_to_all | solution.py:223
  413.7 1.6 copy-done.10
  415.3 1.5 weight_grad.1
  416.7 7.4 %all_to_all.33 = bf16[27,2,8,256]{3,2,0,1:T(8,128)(2,1)S(1)} all-to-all(bf16[27,2,8,256]{3,2,0,1:T(8,128)(2,1)S(1)} %copy.17), channel_id=1, replica_groups=mesh['y'=4,'zh'=2,'zl'=8,'core'=2,'x'=4] {'core'}, dimensions={1} | all-to-all | bytes 442368 | tf_op jit(solution)/shard_map/all_to_all | solution.py:231
  424.1 1.9 collective-permute-start.22
  426.0 32.1 %collective-permute-done.22 = bf16[27,2,8,256]{3,2,0,1:T(8,128)(2,1)S(1)} collective-permute-done((bf16[27,2,8,256]{3,2,0,1:T(8,128)(2,1)S(1)}, bf16[27,2,8,256]{3,2,0,1:T(8,128)(2,1)S(1)}, u32[]{:S(2)}, u32[]{:S(2)}) %collective-permute-start.22) | collective-permute-done | bytes 221216 | tf_op jit(solution)/shard_map/ppermute | solution.py:234
  (93 shorter events, 20.6 us)
Async XLA Ops:
  6.5 102.3 %copy-start.12 = (bf16[2,128,128]{2,1,0:T(8,128)(2,1)S(1)}, bf16[2,128,128]{2,1,0:T(8,128)(2,1)}, u32[]{:S(2)}) copy-start(bf16[2,128,128]{2,1,0:T(8,128)(2,1)} %param.3) | copy-start | bytes 196612
  6.5 102.2 %all-gather.14.cloned.1.call-start = ((), (), s32[]{:S(2)}) async-start(), calls=%async_computation.4 | async-start | bytes 1990656 | tf_op jit(solution)/shard_map/all_gather | solution.py:156
  11.8 34.9 %collective-permute-start.4 = (bf16[27,16,256]{2,1,0:T(8,128)(2,1)S(1)}, bf16[27,16,256]{2,1,0:T(8,128)(2,1)S(1)}, u32[]{:S(2)}, u32[]{:S(2)}) collective-permute-start(bf16[27,16,256]{2,1,0:T(8,128)(2,1)S(1)} %bitcast.40), channel_id=1, source_target_pairs={{0,0},{64,128},{128,256},{192,384},{256,448},{320,320},{384,192},{... | collective-permute-start | bytes 663560 | tf_op jit(solution)/shard_map/ppermute | solution.py:155
  46.7 0.7 copy-start.11
  47.4 147.6 %all-gather.16.cloned.1.call-start = ((), (), s32[]{:S(2)}) async-start(), calls=%async_computation.5 | async-start | bytes 8847360 | tf_op jit(solution)/shard_map/all_gather | solution.py:157
  108.8 304.9 %all-gather.18.cloned.1.call-start = ((), (), s32[]{:S(2)}) async-start(), calls=%async_computation.6 | async-start | bytes 2359296 | tf_op jit(solution)/shard_map/all_gather | solution.py:202
  108.9 11.2 %collective-permute-start.2 = (bf16[128,128]{1,0:T(8,128)(2,1)S(1)}, bf16[128,128]{1,0:T(8,128)(2,1)S(1)}, u32[]{:S(2)}, u32[]{:S(2)}) collective-permute-start(bf16[128,128]{1,0:T(8,128)(2,1)S(1)} %get-tuple-element.60), channel_id=1, source_target_pairs={{0,0},{1,2},{2,4},{3,6},{4,1},{5,3},{6,5},{7,7},{8,8},{9,10},{10,1... | collective-permute-start | bytes 98312 | tf_op jit(solution)/shard_map/ppermute | solution.py:136
  116.8 6.4 %collective-permute-start.3 = (bf16[128,128]{1,0:T(8,128)(2,1)S(1)}, bf16[128,128]{1,0:T(8,128)(2,1)S(1)}, u32[]{:S(2)}, u32[]{:S(2)}) collective-permute-start(bf16[128,128]{1,0:T(8,128)(2,1)S(1)} %get-tuple-element.61), channel_id=1, source_target_pairs={{0,2},{1,0},{2,6},{3,4},{4,3},{5,1},{6,7},{7,5},{8,10},{9,8},{10,1... | collective-permute-start | bytes 98312 | tf_op jit(solution)/shard_map/ppermute | solution.py:136
  195.1 3.0 copy-start
  203.1 0.7 collective-permute-start.5
  203.9 3.0 copy-start.1
  211.4 0.7 collective-permute-start.6
  212.2 3.0 copy-start.2
  219.7 12.9 %collective-permute-start.7 = (bf16[256,128]{1,0:T(8,128)(2,1)S(1)}, bf16[256,128]{1,0:T(8,128)(2,1)S(1)}, u32[]{:S(2)}, u32[]{:S(2)}) collective-permute-start(bf16[256,128]{1,0:T(8,128)(2,1)S(1)} %fusion.13), channel_id=1, source_target_pairs={{256,384},{257,385},{258,386},{259,387},{260,388},{261,389},{262,3... | collective-permute-start | bytes 196616 | tf_op jit(solution)/shard_map/ppermute | solution.py:196
  232.7 3.0 copy-start.3
  240.9 2.6 collective-permute-start.8
  243.5 3.0 copy-start.4
  254.6 0.7 collective-permute-start.9
  255.3 3.0 copy-start.5
  262.9 0.7 collective-permute-start.10
  263.6 3.0 copy-start.6
  271.2 0.7 collective-permute-start.11
  271.9 3.0 copy-start.7
  274.9 16.4 %copy-start.13 = (bf16[2,128,128]{2,1,0:T(8,128)(2,1)S(1)}, bf16[2,128,128]{2,1,0:T(8,128)(2,1)}, u32[]{:S(2)}) copy-start(bf16[2,128,128]{2,1,0:T(8,128)(2,1)} %param.5) | copy-start | bytes 196612
  277.7 8.8 %collective-permute-start.21 = (bf16[256,128]{1,0:T(8,128)(2,1)S(1)}, bf16[256,128]{1,0:T(8,128)(2,1)S(1)}, u32[]{:S(2)}, u32[]{:S(2)}) collective-permute-start(bf16[256,128]{1,0:T(8,128)(2,1)S(1)} %get-tuple-element.50), channel_id=1, source_target_pairs={{0,3},{1,0},{2,1},{3,2},{4,7},{5,4},{6,5},{7,6},{8,11},{9,8},{10,9... | collective-permute-start | bytes 196616 | tf_op jit(solution)/shard_map/ppermute | solution.py:200
  280.9 6.5 %collective-permute-start.20 = (bf16[256,128]{1,0:T(8,128)(2,1)S(1)}, bf16[256,128]{1,0:T(8,128)(2,1)S(1)}, u32[]{:S(2)}, u32[]{:S(2)}) collective-permute-start(bf16[256,128]{1,0:T(8,128)(2,1)S(1)} %get-tuple-element.50), channel_id=1, source_target_pairs={{0,2},{1,3},{2,0},{3,1},{4,6},{5,7},{6,4},{7,5},{8,10},{9,11},{10,... | collective-permute-start | bytes 196616 | tf_op jit(solution)/shard_map/ppermute | solution.py:200
  284.3 6.2 %collective-permute-start.19 = (bf16[256,128]{1,0:T(8,128)(2,1)S(1)}, bf16[256,128]{1,0:T(8,128)(2,1)S(1)}, u32[]{:S(2)}, u32[]{:S(2)}) collective-permute-start(bf16[256,128]{1,0:T(8,128)(2,1)S(1)} %get-tuple-element.50), channel_id=1, source_target_pairs={{0,1},{1,2},{2,3},{3,0},{4,5},{5,6},{6,7},{7,4},{8,9},{9,10},{10,1... | collective-permute-start | bytes 196616 | tf_op jit(solution)/shard_map/ppermute | solution.py:200
  291.3 12.4 %collective-permute-start = (bf16[128,128]{1,0:T(8,128)(2,1)S(1)}, bf16[128,128]{1,0:T(8,128)(2,1)S(1)}, u32[]{:S(2)}, u32[]{:S(2)}) collective-permute-start(bf16[128,128]{1,0:T(8,128)(2,1)S(1)} %get-tuple-element.64), channel_id=1, source_target_pairs={{0,56},{1,58},{2,60},{3,62},{4,57},{5,59},{6,61},{7,63},{8,48},{9,... | collective-permute-start | bytes 98312 | tf_op jit(solution)/shard_map/ppermute | solution.py:136
  300.2 12.1 %collective-permute-start.1 = (bf16[128,128]{1,0:T(8,128)(2,1)S(1)}, bf16[128,128]{1,0:T(8,128)(2,1)S(1)}, u32[]{:S(2)}, u32[]{:S(2)}) collective-permute-start(bf16[128,128]{1,0:T(8,128)(2,1)S(1)} %get-tuple-element.65), channel_id=1, source_target_pairs={{0,58},{1,56},{2,62},{3,60},{4,59},{5,57},{6,63},{7,61},{8,50},{9,... | collective-permute-start | bytes 98312 | tf_op jit(solution)/shard_map/ppermute | solution.py:136
  314.9 3.0 copy-start.8
  319.8 0.7 collective-permute-start.12
  324.4 0.7 collective-permute-start.13
  328.9 0.7 collective-permute-start.14
  332.7 39.6 %collective-permute-start.15 = (bf16[256,128]{1,0:T(8,128)(2,1)S(1)}, bf16[256,128]{1,0:T(8,128)(2,1)S(1)}, u32[]{:S(2)}, u32[]{:S(2)}) collective-permute-start(bf16[256,128]{1,0:T(8,128)(2,1)S(1)} %fusion.18), channel_id=1, source_target_pairs={{120,0},{112,8},{104,16},{96,24},{88,32},{80,40},{72,48},{64,56},{... | collective-permute-start | bytes 196616 | tf_op jit(solution)/shard_map/ppermute | solution.py:214
  374.3 3.0 copy-start.9
  379.1 2.6 collective-permute-start.16
  386.1 0.7 collective-permute-start.17
  390.6 0.7 collective-permute-start.18
  413.7 1.6 copy-start.10
  424.1 34.0 %collective-permute-start.22 = (bf16[27,2,8,256]{3,2,0,1:T(8,128)(2,1)S(1)}, bf16[27,2,8,256]{3,2,0,1:T(8,128)(2,1)S(1)}, u32[]{:S(2)}, u32[]{:S(2)}) collective-permute-start(bf16[27,2,8,256]{3,2,0,1:T(8,128)(2,1)S(1)} %all_to_all.33), channel_id=1, source_target_pairs={{0,0},{128,64},{256,128},{384,192},{448,256},{320,320},{192,384},{... | collective-permute-start | bytes 663560 | tf_op jit(solution)/shard_map/ppermute | solution.py:234
Sparse Core Ops, SparseCore 0:
  47.5 61.1 all-gather.13
  110.9 84.1 all-gather.15
  291.4 76.5 all-gather.17
